TPU v7x, 512 devices: a whole 4x4x16 slice. The times are simulated.
512 devices in a mesh: rows: 32 (over z, core), cols: 16 (over x, y).
Axes of the slice: x: 4, y: 4, z: 16, core: 2. Of those that a mesh axis runs over, the one named last changes fastest.
Arguments:
- matrix: float32 [131072, 4096], P('rows', 'cols'), may hold values from -80 to 80
- mixers: float32 [8, 128, 128], replicated, may hold values from -0.0009765625 to 0.0009765625
- bucket_pair: int32 [1024, 2], P('rows'), may hold values from 0 to 63, all different within a row; in each aligned block of 32 rows (0 to 31, 32 to 63, ...) at most 2 rows name the same one
- mixer_index: int32 [1024], P('rows'), may hold values from 0 to 7
- sign_seed: int32 [1024], P('rows'), may hold values from 0 to 1073741823
Outputs:
- projected: float32 [256, 4096], P('rows', 'cols')
Inputs may be any that keep to these rules, and one draw needn't show every extreme that they name: `bucket_pair`: the two buckets of a tile differ; among the 32 tiles of one device no bucket is named more than 2 times, a bound that some block reaches.
All inputs are finite; a program needn't handle non-finite values.
Results may differ from a plain program's by a relative error of at most 0.0012.
Values may be sent and summed in bfloat16 or wider, within the bound.
A program may use at most 64 MiB of HBM per device.

v0:
```python
import jax
import jax.numpy as jnp
from jax import lax
from jax.sharding import Mesh
from jax.sharding import PartitionSpec as P

TILE = 128
P_SIZE = 256
NB = 64
ROWS = ("rows_0", "rows_1")


def picked(value, axis, root):
    return lax.dynamic_index_in_dim(lax.all_gather(value, axis), root, 0, keepdims=False)


def by_axis(value, axes):
    for axis in axes:
        value = lax.psum(value, axis)
    return value


def row_signs(seed_vals):
    position = jnp.arange(TILE, dtype=jnp.int32)
    hashed = (seed_vals[:, None] ^ position[None, :] * 40503) * 69069
    hashed_bit = hashed >> 16 & 1
    return (1 - 2 * hashed_bit).astype(jnp.float32)


def tile_flips(seed_vals):
    return (1 - 2 * (seed_vals >> 29 & 1)).astype(jnp.float32)


def local(matrix, mixers, bucket_pair, mixer_index, sign_seed):
    col_width = matrix.shape[1]
    tile_count = bucket_pair.shape[0]
    blocks = matrix.reshape(tile_count, TILE, col_width)
    row_sign = row_signs(sign_seed)
    tile_flip = tile_flips(sign_seed).astype(jnp.bfloat16)
    chosen = mixers[mixer_index]
    mixed_tiles = jnp.einsum(
        "tij,tjc->tic",
        chosen,
        row_sign[:, :, None] * blocks,
        precision=lax.Precision.HIGHEST,
        preferred_element_type=jnp.float32,
    ).astype(jnp.bfloat16)
    contrib = jnp.concatenate(
        [mixed_tiles, mixed_tiles * tile_flip[:, None, None]], axis=0
    ).reshape(2 * tile_count, TILE * col_width)
    target = jnp.concatenate([bucket_pair[:, 0], bucket_pair[:, 1]])
    select = (jnp.arange(NB, dtype=jnp.int32)[:, None] == target[None, :]).astype(jnp.bfloat16)
    summed = jnp.dot(select, contrib, preferred_element_type=jnp.float32).reshape(
        1, NB, TILE, col_width
    )
    arrived = lax.all_to_all(summed, ROWS, split_axis=1, concat_axis=0, tiled=True)
    received = jnp.sum(arrived, axis=0)
    sketch = received.reshape(-1, col_width)
    row_parts = lax.axis_size(ROWS)
    panel_owner = picked(sketch, "cols", 0)
    gram_part = jnp.dot(
        panel_owner.T,
        panel_owner,
        precision=lax.Precision.HIGHEST,
        preferred_element_type=jnp.float32,
    )
    cross_part = jnp.dot(
        panel_owner.T, sketch, precision=lax.Precision.HIGHEST, preferred_element_type=jnp.float32
    )
    gram_total, cross_total = (by_axis(gram_part, ROWS), by_axis(cross_part, ROWS))
    factor = jnp.linalg.cholesky(gram_total)
    solved = lax.linalg.triangular_solve(factor, cross_total, left_side=True, lower=True)
    share = P_SIZE // row_parts
    return lax.dynamic_slice_in_dim(solved, lax.axis_index(ROWS) * share, share, 0)


def solution(mesh):
    split = Mesh(mesh.devices.reshape(16, 2, mesh.shape["cols"]), ("rows_0", "rows_1", "cols"))
    return jax.shard_map(
        local,
        mesh=split,
        in_specs=(P(ROWS, "cols"), P(), P(ROWS, None), P(ROWS), P(ROWS)),
        out_specs=P(ROWS, "cols"),
        check_vma=False,
    )
```

profile of v0, /device:TPU:1, one launch (start us, length us, event | category | flops | bytes accessed | tf_op | source)
XLA Modules:
  0.0 730.2 jit_solution(17563179942417183344)
XLA Ops:
  6.5 0.0 copy-start
  6.5 0.0 all-gather.2.cloned.1.call-start
  6.5 0.7 compare_select_fusion
  7.3 0.7 convert_convert_fusion
  7.9 0.7 subtract_convert_fusion
  8.7 0.8 slice_bitcast_fusion.8
  9.4 0.0 copy-done
  9.4 0.7 gather_fusion
  10.1 6.5 broadcast_multiply_fusion
  16.6 0.4 pad_maximum_fusion
  17.0 0.1 pad_add_fusion
  17.1 3.3 fusion.5
  20.4 5.0 copy.17
  25.4 386.9 %all_to_all.12 = f32[1,64,128,256]{3,2,0,1:T(8,128)} all-to-all(f32[1,64,128,256]{3,2,0,1:T(8,128)S(1)} %copy.17), channel_id=1, replica_groups=mesh['rows_0'=16,'rows_1'=2,'cols'=16] {'rows_0','rows_1'}, dimensions={1} | all-to-all | bytes 16777216 | tf_op jit(solution)/shard_map/all_to_all | solution.py:56
  412.3 4.7 reduce_sum.9
  417.0 0.0 all-gather.2.cloned.1.call-update
  417.0 0.0 all-reduce.6.cloned.1.call-start
  417.1 58.3 %all-gather.2.cloned.1.call-done = f32[16,256,256]{2,1,0:T(8,128)} async-done(((f32[1,256,256]{2,1,0:T(8,128)}), f32[16,256,256]{2,1,0:T(8,128)}) %all-gather.2.cloned.1.call-update) | async-done | bytes 4194320 | tf_op jit(solution)/shard_map/all_gather | solution.py:14
  475.4 2.3 fusion.14
  477.7 2.3 fusion.13
  480.0 0.0 all-reduce.6.cloned.1.call-update
  480.1 0.0 all-reduce.8.cloned.1.call-start
  480.1 128.3 %all-reduce.6.cloned.1.call-done = (f32[256,256]{1,0:T(8,128)}, f32[256,256]{0,1:T(8,128)}) async-done(((f32[256,256]{1,0:T(8,128)}, f32[256,256]{0,1:T(8,128)}), (f32[256,256]{1,0:T(8,128)}, f32[256,256]{0,1:T(8,128)})) %all-reduce.6.cloned.1.call-update) | async-done | bytes 524304 | tf_op jit(solution)/shard_map/psum | solution.py:19
  608.4 0.0 all-reduce.8.cloned.1.call-update
  608.5 50.5 %all-reduce.8.cloned.1.call-done = (f32[256,256]{1,0:T(8,128)}, f32[256,256]{0,1:T(8,128)}) async-done(((f32[256,256]{1,0:T(8,128)}, f32[256,256]{0,1:T(8,128)}), (f32[256,256]{1,0:T(8,128)}, f32[256,256]{0,1:T(8,128)})) %all-reduce.8.cloned.1.call-update) | async-done | bytes 524304 | tf_op jit(solution)/shard_map/psum | solution.py:19
  658.9 0.0 copy-start.1
  658.9 1.1 copy.21
  660.1 1.0 fusion.12
  661.1 11.7 %cholesky.50 = f32[128,128]{1,0:T(8,128)S(1)} custom-call(f32[128,128]{1,0:T(8,128)S(1)} %cholesky.118), custom_call_target="Cholesky" | custom-call | tf_op jit(solution)/shard_map/jit(cholesky)/cholesky | solution.py:71
  672.9 9.8 %custom-call.14 = f32[1,128,128]{1,2,0:T(8,128)S(1)} custom-call(f32[1,128,128]{2,1,0:T(8,128)S(1)} %get-tuple-element.30), custom_call_target="InvertDiagBlocksLowerTriangular" | custom-call | tf_op jit(solution)/shard_map/jit(cholesky)/cholesky | solution.py:71
  682.7 0.2 constant_dynamic-update-slice_fusion
  682.9 0.3 convolution_subtract_fusion.1
  683.1 11.7 %cholesky.105 = f32[128,128]{1,0:T(8,128)S(1)} custom-call(f32[128,128]{1,0:T(8,128)S(1)} %convolution_subtract_fusion.1), custom_call_target="Cholesky" | custom-call | tf_op jit(solution)/shard_map/jit(cholesky)/cholesky | solution.py:71
  694.9 0.7 compare_reduce_fusion
  697.0 0.1 triangular_solve.57
  697.1 4.5 while.1
  697.3 0.7 fusion.34
  698.0 1.5 bitcast_dynamic-update-slice_fusion.2
  699.5 0.7 fusion.34
  700.1 1.5 bitcast_dynamic-update-slice_fusion.2
  701.6 19.7 %custom-call.15 = f32[2,128,128]{1,2,0:T(8,128)S(1)} custom-call(f32[2,128,128]{2,1,0:T(8,128)S(1)} %get-tuple-element.12), custom_call_target="InvertDiagBlocksLowerTriangular" | custom-call | tf_op jit(solution)/shard_map/triangular_solve | solution.py:72
  721.3 1.2 fusion.15
  722.5 0.0 copy-done.1
  722.5 0.3 convolution_subtract_fusion
  722.8 0.3 fusion.18
  723.1 0.6 fusion.25
  (11 shorter events, 0.2 us)
Async XLA Ops:
  6.5 2.9 copy-start
  6.5 468.8 %all-gather.2.cloned.1.call-start = ((), (), s32[]{:S(2)}) async-start(), calls=%async_computation.1 | async-start | bytes 4456448 | tf_op jit(solution)/shard_map/all_gather | solution.py:14
  417.0 191.4 %all-reduce.6.cloned.1.call-start = ((), (), s32[]{:S(2)}) async-start(), calls=%async_computation.2 | async-start | bytes 1048576 | tf_op jit(solution)/shard_map/psum | solution.py:19
  480.1 178.9 %all-reduce.8.cloned.1.call-start = ((), (), s32[]{:S(2)}) async-start(), calls=%async_computation.3 | async-start | bytes 1048576 | tf_op jit(solution)/shard_map/psum | solution.py:19
  658.9 63.6 %copy-start.1 = (f32[256,256]{1,0:T(8,128)S(1)}, f32[256,256]{1,0:T(8,128)}, u32[]{:S(2)}) copy-start(f32[256,256]{1,0:T(8,128)} %get-tuple-element.23) | copy-start | bytes 786436
Sparse Core Ops, SparseCore 0:
  417.2 58.1 all-gather.1
  480.2 128.2 all-reduce.5
  611.4 47.5 all-reduce.7
where the time goes:
time: 731 us; the launch traced here: 730 us
  blocking collectives  387 us (53%)
  waiting for transfers between devices  237 us (32%)
  other arithmetic  62.5 us (9%)
  matrix products  16.7 us (2%)
  between operations  14.6 us (2%)
  local copies, waits for them, and re-layouts  12 us (2%)
    all_to_all x1, blocking collectives, local(): lax.all_to_all(summed, ROWS, split_axis=1, concat_axis=0, tiled=True)  387 us
    psum x2, waiting for transfers between devices, by_axis(): value = lax.psum(value, axis)  179 us
    all_gather x1, waiting for transfers between devices, picked(): lax.all_gather(value, axis)  58.3 us
    another operation x6, other arithmetic, local(): factor = jnp.linalg.cholesky(gram_total)  34 us
    another operation x4, other arithmetic, local(): lax.linalg.triangular_solve(factor, cross_total, left_side=True, lower=True)  20.3 us
  transfers between devices with their start and end apart: 3, of which 3 were waited for; matrix products, arithmetic and copies ran while one was open for 0% of the time, Pallas kernels for 0%

commit v1 on v0

v1 whole, which is shorter than its diff:
```python
import functools

import jax
import jax.numpy as jnp
from jax import lax
from jax.experimental import pallas as pl
from jax.experimental.pallas import tpu as pltpu
from jax.sharding import Mesh
from jax.sharding import PartitionSpec as P

TILE = 128
PS = 256
NB = 64
TD = 32
NZ = 16
NK = 2
NX = 4
NC = 16
G = 8
HALF = 128
MESH = pl.DeviceIdType.MESH
HI = lax.Precision.HIGHEST
ROWS = ("z", "k")
COLS = ("x", "y")
F32 = jnp.float32
BF16 = jnp.bfloat16


def place():
    return tuple(lax.axis_index(a) for a in ("z", "k", "x", "y"))


def remote(src, dst, send, recv, to):
    return pltpu.make_async_remote_copy(
        src_ref=src, dst_ref=dst, send_sem=send, recv_sem=recv, device_id=to, device_id_type=MESH
    )


def hello(to):
    pl.semaphore_signal(pltpu.get_barrier_semaphore(), inc=1, device_id=to, device_id_type=MESH)


def meet(count):
    pl.semaphore_wait(pltpu.get_barrier_semaphore(), count)


STEP_TILES = 8


def mix_kernel(which, seeds, mat, mixers, out):
    step = pl.program_id(0)
    lane = lax.broadcasted_iota(jnp.int32, (1, TILE), 1) * 40503
    for pair in range(STEP_TILES // 2):
        parts = []
        for q in range(2):
            here = 2 * pair + q
            tile = step * STEP_TILES + here
            hashed = (seeds[tile] ^ lane) * 69069
            sign = (1 - 2 * ((hashed >> 16) & 1)).astype(F32)
            mixer = mixers[which[tile]] * sign
            block = mat[here * TILE : (here + 1) * TILE, :]
            mixed = jnp.dot(mixer, block, precision=HI, preferred_element_type=F32)
            parts.append(mixed.reshape(TILE // G, G, mixed.shape[1]))
        out[:, pair * 2 * G : (pair + 1) * 2 * G, :] = jnp.concatenate(parts, axis=1).astype(BF16)


def mix(which, seeds, matrix, mixers):
    width = matrix.shape[1]
    return pl.pallas_call(
        mix_kernel,
        out_shape=jax.ShapeDtypeStruct((TILE // G, TD * G, width), BF16),
        grid_spec=pltpu.PrefetchScalarGridSpec(
            num_scalar_prefetch=2,
            grid=(TD // STEP_TILES,),
            in_specs=[
                pl.BlockSpec((STEP_TILES * TILE, width), lambda i, a, b: (i, 0)),
                pl.BlockSpec(mixers.shape, lambda i, a, b: (0, 0, 0)),
            ],
            out_specs=pl.BlockSpec((TILE // G, STEP_TILES * G, width), lambda i, a, b: (0, i, 0)),
        ),
        name="mix",
    )(which, seeds, matrix, mixers)


def scatter_kernel(m_ref, sel_ref, x_ref, other_ref, send, recv, local, sel_sems):
    z, k, x, y = place()
    col = x * NX + y
    source = col == 0
    sibling = {"k": 1 - k}
    hello(sibling)
    for ks in range(NK):
        @pl.when(jnp.logical_not(source))
        def _():
            hello({"k": ks, "x": 0, "y": 0})

    @pl.when(source)
    def _():
        meet(NK * NC - 1)

    @pl.when(jnp.logical_not(source))
    def _():
        meet(1)

    swap = remote(sel_ref, other_ref, sel_sems.at[0], sel_sems.at[1], sibling)
    swap.start()

    def piece(c, kd):
        part = m_ref.at[c, :, pl.ds(pl.multiple_of(kd * HALF, HALF), HALF)]
        return remote(
            part, x_ref.at[k], send.at[c, kd], recv.at[k], {"k": kd, "x": c // NX, "y": c % NX}
        )

    own = pltpu.make_async_copy(
        m_ref.at[0, :, pl.ds(pl.multiple_of(k * HALF, HALF), HALF)], x_ref.at[k], local
    )

    @pl.when(source)
    def _():
        for c in range(1, NC):
            for kd in range(NK):
                piece(c, kd).start()
        piece(0, 1 - k).start()
        own.start()
        own.wait()
        for c in range(1, NC):
            for kd in range(NK):
                piece(c, kd).wait_send()
        piece(0, 1 - k).wait_send()
        remote(x_ref.at[1 - k], x_ref.at[1 - k], send.at[0, 0], recv.at[1 - k], sibling).wait_recv()

    @pl.when(jnp.logical_not(source))
    def _():
        for ks in range(NK):
            remote(x_ref.at[ks], x_ref.at[ks], send.at[0, 0], recv.at[ks], sibling).wait_recv()

    swap.wait()


ANY = pl.BlockSpec(memory_space=pl.ANY)
VM = pl.BlockSpec(memory_space=pltpu.VMEM)
DMA = pltpu.SemaphoreType.DMA


def scatter(mixed, sel):
    return pl.pallas_call(
        scatter_kernel,
        out_shape=(
            jax.ShapeDtypeStruct((NK, TD * G, HALF), BF16),
            jax.ShapeDtypeStruct(sel.shape, BF16),
        ),
        in_specs=[ANY, ANY],
        out_specs=(ANY, ANY),
        scratch_shapes=[DMA((NC, NK)), DMA((NK,)), DMA, DMA((2,))],
        compiler_params=pltpu.CompilerParams(collective_id=1, has_side_effects=True),
        name="scatter",
    )(mixed, sel)


def total_kernel(y_ref, p_ref, got, send_a, recv_a, send_b, recv_b, send_c, recv_c):
    z, k, x, y = place()
    sibling = {"k": 1 - k}
    hello(sibling)
    for d in range(1, NZ):
        hello({"z": lax.rem(z + d, NZ)})
    meet(NZ)
    for d in range(1, NZ):
        zt = lax.rem(z + d, NZ)
        remote(y_ref.at[zt], got.at[d - 1], send_a.at[d - 1], recv_a.at[d - 1], {"z": zt}).start()
    acc = y_ref[z]
    for d in range(1, NZ):
        remote(got.at[d - 1], got.at[d - 1], send_a.at[d - 1], recv_a.at[d - 1], sibling).wait_recv()
        acc = acc + got[d - 1]
    p_ref[k, z] = acc
    for d in range(1, NZ):
        zt = lax.rem(z + d, NZ)
        remote(p_ref.at[k, z], p_ref.at[k, z], send_b.at[d - 1], recv_b.at[d - 1], {"z": zt}).start()

    def hand(d):
        zs = lax.rem(z + NZ - d, NZ)
        return remote(p_ref.at[k, zs], p_ref.at[k, zs], send_c.at[d], recv_c.at[d], sibling)

    hand(0).start()
    for d in range(1, NZ):
        zs = lax.rem(z + NZ - d, NZ)
        remote(p_ref.at[k, zs], p_ref.at[k, zs], send_b.at[d - 1], recv_b.at[d - 1], sibling).wait_recv()
        hand(d).start()
    for d in range(NZ):
        zs = lax.rem(z + NZ - d, NZ)
        remote(
            p_ref.at[1 - k, zs], p_ref.at[1 - k, zs], send_c.at[d], recv_c.at[d], sibling
        ).wait_recv()
    for d in range(1, NZ):
        remote(got.at[d - 1], got.at[d - 1], send_a.at[d - 1], recv_a.at[d - 1], sibling).wait_send()
        remote(p_ref.at[k, z], p_ref.at[k, z], send_b.at[d - 1], recv_b.at[d - 1], sibling).wait_send()
    for d in range(NZ):
        hand(d).wait_send()


def total(part):
    rows = part.shape[0] // NZ
    return pl.pallas_call(
        total_kernel,
        out_shape=jax.ShapeDtypeStruct((NK, NZ, rows, HALF), F32),
        in_specs=[VM],
        out_specs=VM,
        scratch_shapes=[
            pltpu.VMEM((NZ - 1, rows, HALF), F32),
            DMA((NZ - 1,)),
            DMA((NZ - 1,)),
            DMA((NZ - 1,)),
            DMA((NZ - 1,)),
            DMA((NZ,)),
            DMA((NZ,)),
        ],
        compiler_params=pltpu.CompilerParams(collective_id=2, has_side_effects=True),
        name="total",
    )(part.reshape(NZ, rows, HALF))


def share_kernel(w_ref, g_ref, all_ref, gram_ref, got, send_w, recv_w, send_g, recv_g, send_h, recv_h, local):
    z, k, x, y = place()
    col = x * NX + y
    row = z * NK + k
    for c in range(1, NC):
        other = lax.rem(col + c, NC)
        hello({"x": other // NX, "y": lax.rem(other, NX)})
    for d in range(1, NZ * NK):
        other = lax.rem(row + d, NZ * NK)
        hello({"z": other // NK, "k": lax.rem(other, NK)})
    meet(NC - 1 + NZ * NK - 1)

    quarter = PS // 4

    def slot(h, c, s):
        return all_ref.at[c, pl.ds((2 * h + s) * quarter, quarter), :]

    def to(h, stage, direction):
        along_x = (h == 0) == (stage == 0)
        step = 1 if direction == 0 else NX - 1
        if along_x:
            return {"x": lax.rem(x + step, NX)}
        return {"y": lax.rem(y + step, NX)}

    def index(h, a, b):
        if h == 0:
            return lax.rem(x + a, NX) * NX + lax.rem(y + b, NX)
        return lax.rem(x + b, NX) * NX + lax.rem(y + a, NX)

    def move(h, a, b, s, stage, direction, first=None):
        c = index(h, a, b)
        src = slot(h, c, s) if first is None else first
        return remote(src, slot(h, c, s), send_w.at[h, c, s, stage, direction], recv_w.at[h, c, s], to(h, stage, direction))

    def arrived(h, a, b, s):
        c = index(h, a, b)
        remote(
            slot(h, c, s), slot(h, c, s), send_w.at[h, c, s, 0, 0], recv_w.at[h, c, s], {"k": 1 - k}
        ).wait_recv()

    sent = []

    def go(copy):
        copy.start()
        sent.append(copy)

    keep = pltpu.make_async_copy(w_ref, all_ref.at[col], local)
    keep.start()

    own = lambda h, s: w_ref.at[pl.ds((2 * h + s) * quarter, quarter), :]
    for s in range(2):
        for h in range(2):
            go(move(h, 0, 0, s, 0, s, own(h, s)))
    for s in range(2):
        for h in range(2):
            go(move(h, 0, 0, s, 0, 1 - s, own(h, s)))
    grow = pl.multiple_of(row * G, G)
    for c in range(1, NC):
        other = lax.rem(col + c, NC)
        go(
            remote(
                g_ref.at[pl.ds(grow, G), :],
                got.at[c - 1],
                send_g.at[c - 1],
                recv_g.at[c - 1],
                {"x": other // NX, "y": lax.rem(other, NX)},
            )
        )
    for s in range(2):
        for h in range(2):
            go(move(h, 0, 0, s, 1, s, own(h, s)))
    for s in range(2):
        for h in range(2):
            go(move(h, 0, 0, s, 1, 1 - s, own(h, s)))
    for h in range(2):
        arrived(h, 3, 0, 0)
        go(move(h, 3, 0, 0, 0, 0))
        arrived(h, 1, 0, 1)
        go(move(h, 1, 0, 1, 0, 1))
    for h in range(2):
        for a, s in ((3, 0), (1, 1)):
            go(move(h, a, 0, s, 1, s))
            go(move(h, a, 0, s, 1, 1 - s))
    for h in range(2):
        for a, s in ((3, 1), (1, 0)):
            arrived(h, a, 0, s)
            go(move(h, a, 0, s, 1, s))
            go(move(h, a, 0, s, 1, 1 - s))

    acc = g_ref[pl.ds(grow, G), :]
    for c in range(1, NC):
        remote(got.at[c - 1], got.at[c - 1], send_g.at[c - 1], recv_g.at[c - 1], {"k": 1 - k}).wait_recv()
        acc = acc + got[c - 1]
    gram_ref[pl.ds(grow, G), :] = acc
    mine = gram_ref.at[pl.ds(grow, G), :]
    for d in range(1, NZ * NK):
        other = lax.rem(row + d, NZ * NK)
        go(remote(mine, mine, send_h.at[d - 1], recv_h.at[d - 1], {"z": other // NK, "k": lax.rem(other, NK)}))

    for h in range(2):
        for s in range(2):
            arrived(h, 2, 0, s)
            go(move(h, 2, 0, s, 1, s))
            go(move(h, 2, 0, s, 1, 1 - s))
    for a in (0, 3, 1, 2):
        for h in range(2):
            arrived(h, a, 3, 0)
            go(move(h, a, 3, 0, 1, 0))
            arrived(h, a, 1, 1)
            go(move(h, a, 1, 1, 1, 1))
    for h in range(2):
        for a in (0, 3, 1, 2):
            arrived(h, a, 3, 1)
            arrived(h, a, 1, 0)
            for s in range(2):
                arrived(h, a, 2, s)
    for d in range(1, NZ * NK):
        other = lax.rem(row + NZ * NK - d, NZ * NK)
        theirs = gram_ref.at[pl.ds(pl.multiple_of(other * G, G), G), :]
        remote(theirs, theirs, send_h.at[d - 1], recv_h.at[d - 1], {"k": 1 - k}).wait_recv()
    for copy in sent:
        copy.wait_send()
    keep.wait()


def share(block, gram):
    return pl.pallas_call(
        share_kernel,
        out_shape=(
            jax.ShapeDtypeStruct((NC,) + block.shape, F32),
            jax.ShapeDtypeStruct(gram.shape, F32),
        ),
        in_specs=[VM, VM],
        out_specs=(VM, VM),
        scratch_shapes=[
            pltpu.VMEM((NC - 1, G, PS), F32),
            DMA((2, NC, 2, 2, 2)),
            DMA((2, NC, 2)),
            DMA((NC - 1,)),
            DMA((NC - 1,)),
            DMA((NZ * NK - 1,)),
            DMA((NZ * NK - 1,)),
            DMA,
        ],
        compiler_params=pltpu.CompilerParams(collective_id=3, has_side_effects=True),
        name="share",
    )(block, gram)


def finish_kernel(v_ref, o_ref, got, send, recv):
    z, k, x, y = place()
    row = z * NK + k
    parts = NZ * NK
    for d in range(1, parts):
        other = lax.rem(row + d, parts)
        hello({"z": other // NK, "k": lax.rem(other, NK)})
    meet(parts - 1)

    def copy(d):
        other = lax.rem(row + d, parts)
        return remote(
            v_ref.at[pl.ds(pl.multiple_of(other * G, G), G), :],
            got.at[d - 1],
            send.at[d - 1],
            recv.at[d - 1],
            {"z": other // NK, "k": lax.rem(other, NK)},
        )

    for d in range(1, parts):
        copy(d).start()
    acc = v_ref[pl.ds(pl.multiple_of(row * G, G), G), :]
    for d in range(1, parts):
        copy(d).wait_recv()
        acc = acc + got[d - 1]
    o_ref[...] = acc
    for d in range(1, parts):
        copy(d).wait_send()


def finish(value):
    parts = NZ * NK
    return pl.pallas_call(
        finish_kernel,
        out_shape=jax.ShapeDtypeStruct((G, value.shape[1]), F32),
        in_specs=[VM],
        out_specs=VM,
        scratch_shapes=[pltpu.VMEM((parts - 1, G, value.shape[1]), F32), DMA((parts - 1,)), DMA((parts - 1,))],
        compiler_params=pltpu.CompilerParams(collective_id=4, has_side_effects=True),
        name="finish",
    )(value)


def spread(sel):
    eye = jnp.eye(G, dtype=BF16)
    return (sel[:, None, :, None] * eye[None, :, None, :]).reshape(NB * G, TD * G)


def local(matrix, mixers, bucket_pair, mixer_index, sign_seed):
    mixed = mix(mixer_index, sign_seed, matrix, mixers)
    flip = (1 - 2 * (sign_seed >> 29 & 1)).astype(F32)
    bucket = jnp.arange(NB, dtype=jnp.int32)[:, None]
    sel = (bucket == bucket_pair[:, 0]).astype(F32) + flip * (bucket == bucket_pair[:, 1]).astype(F32)
    sel = sel.astype(BF16)
    panel, other = scatter(mixed, jnp.pad(sel, ((0, 0), (0, HALF - TD))))
    core = lax.axis_index("k")
    mine = spread(sel)
    theirs = spread(other[:, :TD])
    both = jnp.where(core == 0, jnp.concatenate([mine, theirs], 1), jnp.concatenate([theirs, mine], 1))
    part = jnp.dot(both, panel.reshape(NK * TD * G, HALF), preferred_element_type=F32)
    sketch = total(part).reshape(NK, NB * G, HALF)
    sketch = jnp.concatenate([sketch[0], sketch[1]], axis=1)
    weight = jnp.dot(mine.T.astype(F32), sketch, precision=HI, preferred_element_type=F32)
    gram_part = jnp.dot(sketch.T, sketch, precision=HI, preferred_element_type=F32)
    weights, gram = share(weight, gram_part)
    cross = jnp.dot(
        weights.reshape(NC * TD * G, PS).T,
        mixed.reshape(NC * TD * G, PS).astype(F32),
        precision=HI,
        preferred_element_type=F32,
    )
    factor = jnp.linalg.cholesky(gram)
    solved = lax.linalg.triangular_solve(factor, cross, left_side=True, lower=True)
    return finish(solved)


def solution(mesh):
    split = Mesh(mesh.devices.reshape(NZ, NK, NX, NX), ("z", "k", "x", "y"))
    return jax.shard_map(
        local,
        mesh=split,
        in_specs=(P(ROWS, COLS), P(), P(ROWS, None), P(ROWS), P(ROWS)),
        out_specs=P(ROWS, COLS),
        check_vma=False,
    )
```

time: 731 us -> 251 us (0.34)
  blocking collectives: 387 us -> 0 us
  waiting for transfers between devices: 237 us -> 0 us
  Pallas kernels: 0 us -> 150 us
  local copies, waits for them, and re-layouts: 12 us -> 28.6 us
  between operations: 14.6 us -> 1.47 us
    all_to_all x1 -> x0, blocking collectives: 387 us -> none  [local(): lax.all_to_all(summed, ROWS, split_axis=1, concat_axis=0, tiled=True)]
    psum x2 -> x0, waiting for transfers between devices: 179 us -> none  [by_axis(): value = lax.psum(value, axis)]
    pallas_call x0 -> x5, Pallas kernels: none -> 150 us  [the longest x1 44.7 us: total(): pl.pallas_call(total_kernel, out_shape=jax.ShapeDtypeStruct((NK, NZ, rows...]
    all_gather x1 -> x0, waiting for transfers between devices: 58.3 us -> none  [picked(): lax.all_gather(value, axis)]
    mul x0 -> x3, local copies, waits for them, and re-layouts: none -> 20.7 us  [spread(): sel[:, None, :, None] * eye[None, :, None, :]]
  transfers between devices with their start and end apart: 3 -> 0, of which waited for: 3 -> 0; matrix products, arithmetic and copies ran while one was open for 0% -> 0% of each run, Pallas kernels for 0% -> 0%
where the time goes in v1:
time: 251 us; the launch traced here: 250 us
  Pallas kernels  150 us (60%)
  other arithmetic  59.6 us (24%)
  local copies, waits for them, and re-layouts  28.6 us (11%)
  matrix products  10.9 us (4%)
    pallas_call x1, Pallas kernels, total(): pl.pallas_call(total_kernel, out_shape=jax.ShapeDtypeStruct((NK, NZ, rows...  44.7 us
    pallas_call x1, Pallas kernels, share(): pl.pallas_call(share_kernel, out_shape=(jax.ShapeDtypeStruct((NC,) + bloc...  41.9 us
    another operation x6, other arithmetic, local(): factor = jnp.linalg.cholesky(gram)  34.2 us
    pallas_call x1, Pallas kernels, scatter(): pl.pallas_call(scatter_kernel, out_shape=(jax.ShapeDtypeStruct((NK, TD *...  30.7 us
    pallas_call x1, Pallas kernels, finish(): pl.pallas_call(finish_kernel, out_shape=jax.ShapeDtypeStruct((G, value.sh...  25 us
    mul x3, local copies, waits for them, and re-layouts, spread(): sel[:, None, :, None] * eye[None, :, None, :]  20.7 us
    another operation x4, other arithmetic, local(): lax.linalg.triangular_solve(factor, cross, left_side=True, lower=True)  20.4 us
    pallas_call x1, Pallas kernels, mix(): pl.pallas_call(mix_kernel, out_shape=jax.ShapeDtypeStruct((TILE // G, TD...  7.41 us

profile of v1, /device:TPU:1, one launch (start us, length us, event | category | flops | bytes accessed | tf_op | source)
XLA Modules:
  0.0 250.4 jit_solution(17562787549941213398)
XLA Ops:
  0.0 0.7 subtract_convert_fusion
  0.7 0.1 triangular_solve.57
  0.7 0.8 slice_bitcast_fusion.5
  1.5 0.6 pad.5.sel_ref
  2.1 7.4 %mix.1.m_ref = bf16[16,256,256]{2,1,0:T(8,128)(2,1)} custom-call(s32[32]{0:T(128)} %which.1, s32[32]{0:T(128)} %seeds.1, f32[4096,256]{1,0:T(8,128)} %mat.1, f32[8,128,128]{2,1,0:T(8,128)} %mixers.1), custom_call_target="tpu_custom_call" | custom-call | tf_op jit(solution)/shard_map/mix/pallas_call | solution.py:69
  9.5 30.7 %scatter.1 = (bf16[2,256,128]{2,1,0:T(8,128)(2,1)}, bf16[64,128]{1,0:T(8,128)(2,1)}) custom-call(bf16[16,256,256]{2,1,0:T(8,128)(2,1)} %mix.1.m_ref, bf16[64,128]{1,0:T(8,128)(2,1)} %pad.5.sel_ref), custom_call_target="tpu_custom_call" | custom-call | tf_op jit(solution)/shard_map/scatter/pallas_call | solution.py:145
  40.2 4.2 %broadcast_multiply_fusion = (bf16[64,8,32,8]{3,2,1,0:T(8,128)(2,1)}, bf16[64,8,32,8]{3,2,1,0:T(8,128)(2,1)}) fusion(bf16[64,32]{1,0:T(8,128)(2,1)} %bitcast.57, bf16[8,8]{1,0:T(8,128)(2,1)S(1)} %fusion.17, bf16[64,32]{1,0:T(8,128)(2,1)S(1)} %add_convert_fusion), kind=kLoop, calls=%fused_computation.2 | loop fusion | flops 262144 | bytes 532608 | tf_op jit(solution)/shard_map/mul | solution.py:414
  44.5 6.9 %mul.64 = bf16[16,32,256]{2,1,0:T(8,128)(2,1)S(1)} reshape(bf16[64,8,32,8]{3,2,1,0:T(8,128)(2,1)} %get-tuple-element.37) | data formatting | bytes 524288 | tf_op jit(solution)/shard_map/mul | solution.py:414
  51.4 0.0 copy-start.2
  51.4 6.9 %mul.61 = bf16[16,32,256]{2,1,0:T(8,128)(2,1)S(1)} reshape(bf16[64,8,32,8]{3,2,1,0:T(8,128)(2,1)} %get-tuple-element.38) | data formatting | bytes 524288 | tf_op jit(solution)/shard_map/mul | solution.py:414
  58.3 6.9 %mul.60 = bf16[512,256]{1,0:T(8,128)(2,1)S(1)} reshape(bf16[64,8,32,8]{3,2,1,0:T(8,128)(2,1)} %get-tuple-element.38) | data formatting | bytes 524288 | tf_op jit(solution)/shard_map/mul | solution.py:414
  65.2 0.0 copy-done.2
  65.2 0.0 copy-start
  65.2 1.0 fusion.y_ref
  66.3 44.7 %total.1 = f32[2,16,32,128]{3,2,1,0:T(8,128)} custom-call(f32[16,32,128]{2,1,0:T(8,128)} %fusion.y_ref), custom_call_target="tpu_custom_call" | custom-call | tf_op jit(solution)/shard_map/total/pallas_call | solution.py:201
  110.9 1.1 fusion.22
  112.0 1.2 fusion.8.w_ref
  113.2 1.7 fusion.7.g_ref
  114.9 41.9 %share.1 = (f32[16,256,256]{2,1,0:T(8,128)}, f32[256,256]{1,0:T(8,128)}) custom-call(f32[256,256]{1,0:T(8,128)} %fusion.8.w_ref, f32[256,256]{1,0:T(8,128)} %fusion.7.g_ref), custom_call_target="tpu_custom_call" | custom-call | tf_op jit(solution)/shard_map/share/pallas_call | solution.py:346
  156.9 0.0 copy-start.1
  156.9 0.0 copy-done
  156.9 5.6 %convolution_bitcast_fusion = f32[256,256]{1,0:T(8,128)S(1)} fusion(f32[16,256,256]{2,1,0:T(8,128)} %get-tuple-element.12, bf16[16,256,256]{2,1,0:T(8,128)(2,1)S(1)} %copy-done), kind=kOutput, calls=%fused_computation.4 | convolution fusion | flops 3221225472 | bytes 6553600 | tf_op jit(solution)/shard_map/dot_general | solution.py:434
  162.5 0.0 copy-done.1
  162.6 0.1 copy.8
  162.7 11.7 %cholesky.50 = f32[128,128]{1,0:T(8,128)S(1)} custom-call(f32[128,128]{1,0:T(8,128)S(1)} %cholesky.118), custom_call_target="Cholesky" | custom-call | tf_op jit(solution)/shard_map/jit(cholesky)/cholesky | solution.py:440
  174.5 9.8 %custom-call.14 = f32[1,128,128]{1,2,0:T(8,128)S(1)} custom-call(f32[1,128,128]{2,1,0:T(8,128)S(1)} %get-tuple-element.36), custom_call_target="InvertDiagBlocksLowerTriangular" | custom-call | tf_op jit(solution)/shard_map/jit(cholesky)/cholesky | solution.py:440
  184.3 0.2 constant_dynamic-update-slice_fusion.1
  184.6 0.3 convolution_subtract_fusion.1
  184.8 11.9 %cholesky.105 = f32[128,128]{1,0:T(8,128)S(1)} custom-call(f32[128,128]{1,0:T(8,128)S(1)} %convolution_subtract_fusion.1), custom_call_target="Cholesky" | custom-call | tf_op jit(solution)/shard_map/jit(cholesky)/cholesky | solution.py:440
  196.8 0.7 compare_reduce_fusion
  198.7 4.0 %while.1 = (s32[]{:T(128)}, f32[256,256]{1,0:T(8,128)S(1)}, s32[2,2]{1,0:T(2,128)S(1)}, f32[2,128,128]{2,1,0:T(8,128)S(1)}, s32[]{:T(128)}) while((s32[]{:T(128)}, f32[256,256]{1,0:T(8,128)S(1)}, s32[2,2]{1,0:T(2,128)S(1)}, f32[2,128,128]{2,1,0:T(8,128)S(1)}, s32[]{:T(128)}) %tuple.26), condition=%wide.while_cond, body=%wide.while_body.sunk | while | flops 2 | bytes 131189 | solution.py:441
  198.8 0.6 fusion.32
  199.4 1.3 bitcast_dynamic-update-slice_fusion.2
  200.8 0.6 fusion.32
  201.4 1.3 bitcast_dynamic-update-slice_fusion.2
  202.8 19.7 %custom-call.15 = f32[2,128,128]{1,2,0:T(8,128)S(1)} custom-call(f32[2,128,128]{2,1,0:T(8,128)S(1)} %get-tuple-element.20), custom_call_target="InvertDiagBlocksLowerTriangular" | custom-call | tf_op jit(solution)/shard_map/triangular_solve | solution.py:441
  222.5 0.3 fusion.10
  222.8 0.3 convolution_subtract_fusion
  223.0 0.3 fusion.13
  223.4 0.7 pad_maximum_fusion.3.v_ref
  224.1 25.0 %finish.1 = f32[8,256]{1,0:T(8,128)} custom-call(f32[256,256]{1,0:T(8,128)} %pad_maximum_fusion.3.v_ref), custom_call_target="tpu_custom_call" | custom-call | tf_op jit(solution)/shard_map/finish/pallas_call | solution.py:401
  249.1 1.3 copy.23
  (12 shorter events, 0.2 us)
Async XLA Ops:
  51.4 13.8 %copy-start.2 = (bf16[2,256,128]{2,1,0:T(8,128)(2,1)S(1)}, bf16[2,256,128]{2,1,0:T(8,128)(2,1)}, u32[]{:S(2)}) copy-start(bf16[2,256,128]{2,1,0:T(8,128)(2,1)} %get-tuple-element.10) | copy-start | bytes 393220
  65.2 91.6 %copy-start = (bf16[16,256,256]{2,1,0:T(8,128)(2,1)S(1)}, bf16[16,256,256]{2,1,0:T(8,128)(2,1)}, u32[]{:S(2)}) copy-start(bf16[16,256,256]{2,1,0:T(8,128)(2,1)} %mix.1.m_ref) | copy-start | bytes 6291460
  156.9 5.7 %copy-start.1 = (f32[256,256]{1,0:T(8,128)S(1)}, f32[256,256]{1,0:T(8,128)}, u32[]{:S(2)}) copy-start(f32[256,256]{1,0:T(8,128)} %get-tuple-element.11) | copy-start | bytes 786436

commit v2 on v1

--- a/solution.py
+++ b/solution.py
@@ -44,10 +44,14 @@
     pl.semaphore_wait(pltpu.get_barrier_semaphore(), count)
 
 
+def dot(a, b):
+    return jnp.dot(a, b, precision=HI, preferred_element_type=F32)
+
+
 STEP_TILES = 8
 
 
-def mix_kernel(which, seeds, mat, mixers, out):
+def mix_kernel(which, seeds, pairs, mat, mixers, out, meta):
     step = pl.program_id(0)
     lane = lax.broadcasted_iota(jnp.int32, (1, TILE), 1) * 40503
     for pair in range(STEP_TILES // 2):
@@ -63,23 +67,53 @@
             parts.append(mixed.reshape(TILE // G, G, mixed.shape[1]))
         out[:, pair * 2 * G : (pair + 1) * 2 * G, :] = jnp.concatenate(parts, axis=1).astype(BF16)
 
-
-def mix(which, seeds, matrix, mixers):
+    @pl.when(step == 0)
+    def _():
+        tiles = lax.broadcasted_iota(jnp.int32, (1, TD * G), 1) // G
+        first = jnp.zeros((1, TD * G), jnp.int32)
+        second, seed = first, first
+        for t in range(TD):
+            first = jnp.where(tiles == t, pairs[2 * t], first)
+            second = jnp.where(tiles == t, pairs[2 * t + 1], second)
+            seed = jnp.where(tiles == t, seeds[t], seed)
+        flip = 1 - 2 * (seed >> 29 & 1)
+        row = lax.broadcasted_iota(jnp.int32, (G, TD * G), 0)
+        meta[...] = jnp.where(row == 0, first, jnp.where(row == 1, second, flip)).astype(F32)
+
+
+def mix(which, seeds, pairs, matrix, mixers):
     width = matrix.shape[1]
     return pl.pallas_call(
         mix_kernel,
-        out_shape=jax.ShapeDtypeStruct((TILE // G, TD * G, width), BF16),
+        out_shape=(
+            jax.ShapeDtypeStruct((TILE // G, TD * G, width), BF16),
+            jax.ShapeDtypeStruct((G, TD * G), F32),
+        ),
         grid_spec=pltpu.PrefetchScalarGridSpec(
-            num_scalar_prefetch=2,
+            num_scalar_prefetch=3,
             grid=(TD // STEP_TILES,),
             in_specs=[
-                pl.BlockSpec((STEP_TILES * TILE, width), lambda i, a, b: (i, 0)),
-                pl.BlockSpec(mixers.shape, lambda i, a, b: (0, 0, 0)),
+                pl.BlockSpec((STEP_TILES * TILE, width), lambda i, a, b, c: (i, 0)),
+                pl.BlockSpec(mixers.shape, lambda i, a, b, c: (0, 0, 0)),
             ],
-            out_specs=pl.BlockSpec((TILE // G, STEP_TILES * G, width), lambda i, a, b: (0, i, 0)),
+            out_specs=(
+                pl.BlockSpec((TILE // G, STEP_TILES * G, width), lambda i, a, b, c: (0, i, 0)),
+                pl.BlockSpec((G, TD * G), lambda i, a, b, c: (0, 0)),
+            ),
         ),
         name="mix",
-    )(which, seeds, matrix, mixers)
+    )(which, seeds, pairs, matrix, mixers)
+
+
+def selection(meta):
+    row = lax.broadcasted_iota(jnp.int32, (NB * G, TD * G), 0)
+    lane = lax.broadcasted_iota(jnp.int32, (NB * G, TD * G), 1)
+    first = meta[0:1, :].astype(jnp.int32)
+    second = meta[1:2, :].astype(jnp.int32)
+    flip = meta[2:3, :]
+    bucket = row >> 3
+    value = jnp.where(bucket == first, 1.0, 0.0) + jnp.where(bucket == second, flip, 0.0)
+    return jnp.where((row & 7) == (lane & 7), value, 0.0).astype(BF16)
 
 
 def scatter_kernel(m_ref, sel_ref, x_ref, other_ref, send, recv, local, sel_sems):
@@ -146,7 +180,7 @@
         scatter_kernel,
         out_shape=(
             jax.ShapeDtypeStruct((NK, TD * G, HALF), BF16),
-            jax.ShapeDtypeStruct(sel.shape, BF16),
+            jax.ShapeDtypeStruct(sel.shape, F32),
         ),
         in_specs=[ANY, ANY],
         out_specs=(ANY, ANY),
@@ -156,12 +190,15 @@
     )(mixed, sel)
 
 
-def total_kernel(y_ref, p_ref, got, send_a, recv_a, send_b, recv_b, send_c, recv_c):
+def total_kernel(x_ref, mine_ref, other_ref, p_ref, y_ref, got, send_a, recv_a, send_b, recv_b, send_c, recv_c):
     z, k, x, y = place()
     sibling = {"k": 1 - k}
     hello(sibling)
     for d in range(1, NZ):
         hello({"z": lax.rem(z + d, NZ)})
+    part = jnp.dot(selection(mine_ref[...]), x_ref[k], preferred_element_type=F32)
+    part = part + jnp.dot(selection(other_ref[...]), x_ref[1 - k], preferred_element_type=F32)
+    y_ref[...] = part.reshape(y_ref.shape)
     meet(NZ)
     for d in range(1, NZ):
         zt = lax.rem(z + d, NZ)
@@ -196,14 +233,15 @@
         hand(d).wait_send()
 
 
-def total(part):
-    rows = part.shape[0] // NZ
+def total(panel, mine, other):
+    rows = NB * G // NZ
     return pl.pallas_call(
         total_kernel,
         out_shape=jax.ShapeDtypeStruct((NK, NZ, rows, HALF), F32),
-        in_specs=[VM],
+        in_specs=[VM, VM, VM],
         out_specs=VM,
         scratch_shapes=[
+            pltpu.VMEM((NZ, rows, HALF), F32),
             pltpu.VMEM((NZ - 1, rows, HALF), F32),
             DMA((NZ - 1,)),
             DMA((NZ - 1,)),
@@ -214,20 +252,28 @@
         ],
         compiler_params=pltpu.CompilerParams(collective_id=2, has_side_effects=True),
         name="total",
-    )(part.reshape(NZ, rows, HALF))
-
-
-def share_kernel(w_ref, g_ref, all_ref, gram_ref, got, send_w, recv_w, send_g, recv_g, send_h, recv_h, local):
+    )(panel, mine, other)
+
+
+def share_kernel(p_ref, meta_ref, all_ref, gram_ref, w_ref, g_ref, got, send_w, recv_w, send_g, recv_g, send_h, recv_h, local):
     z, k, x, y = place()
     col = x * NX + y
-    row = z * NK + k
-    for c in range(1, NC):
-        other = lax.rem(col + c, NC)
-        hello({"x": other // NX, "y": lax.rem(other, NX)})
-    for d in range(1, NZ * NK):
-        other = lax.rem(row + d, NZ * NK)
-        hello({"z": other // NK, "k": lax.rem(other, NK)})
-    meet(NC - 1 + NZ * NK - 1)
+
+    def plane(d):
+        other = lax.rem(k * NC + col + d, NK * NC)
+        c = lax.rem(other, NC)
+        return other // NC, c, {"k": other // NC, "x": c // NX, "y": lax.rem(c, NX)}
+
+    for d in range(1, NK * NC):
+        hello(plane(d)[2])
+    sketch = jnp.concatenate([p_ref[0].reshape(NB * G, HALF), p_ref[1].reshape(NB * G, HALF)], axis=1)
+    turned = sketch.T
+    g_ref[...] = dot(turned, sketch)
+    w_ref[...] = dot(turned, selection(meta_ref[...]).astype(F32))
+    meet(NK * NC - 1)
+
+    def rows_of(kk, c):
+        return pl.ds(pl.multiple_of(kk * HALF + c * G, G), G)
 
     quarter = PS // 4
 
@@ -263,6 +309,17 @@
         copy.start()
         sent.append(copy)
 
+    for d in range(1, NC):
+        c = lax.rem(col + d, NC)
+        go(
+            remote(
+                g_ref.at[rows_of(k, c), :],
+                got.at[d - 1],
+                send_g.at[d - 1],
+                recv_g.at[d - 1],
+                {"x": c // NX, "y": lax.rem(c, NX)},
+            )
+        )
     keep = pltpu.make_async_copy(w_ref, all_ref.at[col], local)
     keep.start()
 
@@ -273,18 +330,6 @@
     for s in range(2):
         for h in range(2):
             go(move(h, 0, 0, s, 0, 1 - s, own(h, s)))
-    grow = pl.multiple_of(row * G, G)
-    for c in range(1, NC):
-        other = lax.rem(col + c, NC)
-        go(
-            remote(
-                g_ref.at[pl.ds(grow, G), :],
-                got.at[c - 1],
-                send_g.at[c - 1],
-                recv_g.at[c - 1],
-                {"x": other // NX, "y": lax.rem(other, NX)},
-            )
-        )
     for s in range(2):
         for h in range(2):
             go(move(h, 0, 0, s, 1, s, own(h, s)))
@@ -306,15 +351,14 @@
             go(move(h, a, 0, s, 1, s))
             go(move(h, a, 0, s, 1, 1 - s))
 
-    acc = g_ref[pl.ds(grow, G), :]
-    for c in range(1, NC):
-        remote(got.at[c - 1], got.at[c - 1], send_g.at[c - 1], recv_g.at[c - 1], {"k": 1 - k}).wait_recv()
-        acc = acc + got[c - 1]
-    gram_ref[pl.ds(grow, G), :] = acc
-    mine = gram_ref.at[pl.ds(grow, G), :]
-    for d in range(1, NZ * NK):
-        other = lax.rem(row + d, NZ * NK)
-        go(remote(mine, mine, send_h.at[d - 1], recv_h.at[d - 1], {"z": other // NK, "k": lax.rem(other, NK)}))
+    acc = g_ref[rows_of(k, col), :]
+    for d in range(1, NC):
+        remote(got.at[d - 1], got.at[d - 1], send_g.at[d - 1], recv_g.at[d - 1], {"k": 1 - k}).wait_recv()
+        acc = acc + got[d - 1]
+    gram_ref[rows_of(k, col), :] = acc
+    mine = gram_ref.at[rows_of(k, col), :]
+    for d in range(1, NK * NC):
+        go(remote(mine, mine, send_h.at[d - 1], recv_h.at[d - 1], plane(d)[2]))
 
     for h in range(2):
         for s in range(2):
@@ -333,113 +377,173 @@
             arrived(h, a, 1, 0)
             for s in range(2):
                 arrived(h, a, 2, s)
-    for d in range(1, NZ * NK):
-        other = lax.rem(row + NZ * NK - d, NZ * NK)
-        theirs = gram_ref.at[pl.ds(pl.multiple_of(other * G, G), G), :]
+    for d in range(1, NK * NC):
+        kk, c, where = plane(NK * NC - d)
+        theirs = gram_ref.at[rows_of(kk, c), :]
         remote(theirs, theirs, send_h.at[d - 1], recv_h.at[d - 1], {"k": 1 - k}).wait_recv()
     for copy in sent:
         copy.wait_send()
     keep.wait()
 
 
-def share(block, gram):
+def share(sketch, meta):
     return pl.pallas_call(
         share_kernel,
         out_shape=(
-            jax.ShapeDtypeStruct((NC,) + block.shape, F32),
-            jax.ShapeDtypeStruct(gram.shape, F32),
+            jax.ShapeDtypeStruct((NC, PS, TD * G), F32),
+            jax.ShapeDtypeStruct((PS, PS), F32),
         ),
         in_specs=[VM, VM],
         out_specs=(VM, VM),
         scratch_shapes=[
+            pltpu.VMEM((PS, TD * G), F32),
+            pltpu.VMEM((PS, PS), F32),
             pltpu.VMEM((NC - 1, G, PS), F32),
             DMA((2, NC, 2, 2, 2)),
             DMA((2, NC, 2)),
             DMA((NC - 1,)),
             DMA((NC - 1,)),
-            DMA((NZ * NK - 1,)),
-            DMA((NZ * NK - 1,)),
+            DMA((NK * NC - 1,)),
+            DMA((NK * NC - 1,)),
             DMA,
         ],
         compiler_params=pltpu.CompilerParams(collective_id=3, has_side_effects=True),
         name="share",
-    )(block, gram)
-
-
-def finish_kernel(v_ref, o_ref, got, send, recv):
+    )(sketch, meta)
+
+
+NBK = 64
+
+
+def invert_block(block):
+    n = NBK
+    ident = (lax.broadcasted_iota(jnp.int32, (n, n), 0) == lax.broadcasted_iota(jnp.int32, (n, n), 1)).astype(F32)
+    aug = jnp.concatenate([block, ident], axis=1)
+    groups = n // G
+    rows = [aug[g * G : (g + 1) * G, :] for g in range(groups)]
+    sub = lax.broadcasted_iota(jnp.int32, (G, 2 * n), 0)
+    for g in range(groups):
+        cols = [
+            {h: jnp.broadcast_to(rows[h][:, g * G + i : g * G + i + 1], (G, 2 * n)) for h in range(g, groups)}
+            for i in range(G)
+        ]
+        scale = jnp.zeros((G, 2 * n), F32)
+        for i in range(G):
+            pivot = jnp.broadcast_to(cols[i][g][i : i + 1, :], (G, 2 * n))
+            inv = 1.0 / pivot
+            scale = jnp.where(sub == i, lax.rsqrt(pivot), scale)
+            below = dict(cols[i])
+            below[g] = jnp.where(sub > i, below[g], 0.0)
+            for m in range(i + 1, G):
+                f = jnp.broadcast_to(cols[m][g][i : i + 1, :], (G, 2 * n)) * inv
+                for h in range(g, groups):
+                    cols[m][h] = cols[m][h] - below[h] * f
+            u = jnp.broadcast_to(rows[g][i : i + 1, :], (G, 2 * n)) * inv
+            for h in range(g, groups):
+                rows[h] = rows[h] - below[h] * u
+        rows[g] = rows[g] * scale
+    done = jnp.concatenate(rows, axis=0)
+    return done[:, n:]
+
+
+def inverse_factor(gram_ref, work):
+    n = PS
+    work[:, :n] = gram_ref[...]
+    work[:, n:] = (lax.broadcasted_iota(jnp.int32, (n, n), 0) == lax.broadcasted_iota(jnp.int32, (n, n), 1)).astype(F32)
+    for p in range(n // NBK):
+        lo, hi = p * NBK, (p + 1) * NBK
+        inv = invert_block(work[lo:hi, lo:hi])
+        row = dot(inv, work[lo:hi, :])
+        work[lo:hi, :] = row
+        if hi < n:
+            work[hi:, :] = work[hi:, :] - dot(row[:, hi:n].T, row)
+
+
+def factor_kernel(gram_ref, out, work):
+    inverse_factor(gram_ref, work)
+    out[...] = work[:, PS:]
+
+
+def factor(gram):
+    return pl.pallas_call(
+        factor_kernel,
+        out_shape=jax.ShapeDtypeStruct((PS, PS), F32),
+        in_specs=[VM],
+        out_specs=VM,
+        scratch_shapes=[pltpu.VMEM((PS, 2 * PS), F32)],
+        name="factor",
+    )(gram)
+
+
+def finish_kernel(w_ref, m_ref, inv_ref, o_ref, value, summed, pair, got, send, recv, pair_sems):
     z, k, x, y = place()
-    row = z * NK + k
-    parts = NZ * NK
-    for d in range(1, parts):
-        other = lax.rem(row + d, parts)
-        hello({"z": other // NK, "k": lax.rem(other, NK)})
-    meet(parts - 1)
+    sibling = {"k": 1 - k}
+    hello(sibling)
+    for d in range(1, NZ):
+        hello({"z": lax.rem(z + d, NZ)})
+
+    def add(c, acc):
+        w = w_ref[c]
+        high = w.astype(BF16)
+        rest = w - high.astype(F32)
+        low = rest.astype(BF16)
+        last = (rest - low.astype(F32)).astype(BF16)
+        m = m_ref[c]
+        for part in (high, low, last):
+            acc = acc + jnp.dot(part, m, preferred_element_type=F32)
+        return acc
+
+    cross = lax.fori_loop(0, NC, add, jnp.zeros((PS, m_ref.shape[2]), F32))
+    value[...] = dot(inv_ref[...], cross).reshape(value.shape)
+    meet(NZ)
+    swap = remote(value.at[:, 1 - k], pair, pair_sems.at[0], pair_sems.at[1], sibling)
+    swap.start()
+    swap.wait_recv()
+    summed[...] = value[:, k] + pair[...]
 
     def copy(d):
-        other = lax.rem(row + d, parts)
-        return remote(
-            v_ref.at[pl.ds(pl.multiple_of(other * G, G), G), :],
-            got.at[d - 1],
-            send.at[d - 1],
-            recv.at[d - 1],
-            {"z": other // NK, "k": lax.rem(other, NK)},
-        )
-
-    for d in range(1, parts):
+        zt = lax.rem(z + d, NZ)
+        return remote(summed.at[zt], got.at[d - 1], send.at[d - 1], recv.at[d - 1], {"z": zt})
+
+    for d in range(1, NZ):
         copy(d).start()
-    acc = v_ref[pl.ds(pl.multiple_of(row * G, G), G), :]
-    for d in range(1, parts):
+    acc = summed[z]
+    for d in range(1, NZ):
         copy(d).wait_recv()
         acc = acc + got[d - 1]
     o_ref[...] = acc
-    for d in range(1, parts):
+    for d in range(1, NZ):
         copy(d).wait_send()
-
-
-def finish(value):
-    parts = NZ * NK
+    swap.wait_send()
+
+
+def finish(weights, mixed, inverse):
+    width = mixed.shape[2]
     return pl.pallas_call(
         finish_kernel,
-        out_shape=jax.ShapeDtypeStruct((G, value.shape[1]), F32),
-        in_specs=[VM],
+        out_shape=jax.ShapeDtypeStruct((G, width), F32),
+        in_specs=[VM, VM, VM],
         out_specs=VM,
-        scratch_shapes=[pltpu.VMEM((parts - 1, G, value.shape[1]), F32), DMA((parts - 1,)), DMA((parts - 1,))],
+        scratch_shapes=[
+            pltpu.VMEM((NZ, NK, G, width), F32),
+            pltpu.VMEM((NZ, G, width), F32),
+            pltpu.VMEM((NZ, G, width), F32),
+            pltpu.VMEM((NZ - 1, G, width), F32),
+            DMA((NZ - 1,)),
+            DMA((NZ - 1,)),
+            DMA((2,)),
+        ],
         compiler_params=pltpu.CompilerParams(collective_id=4, has_side_effects=True),
         name="finish",
-    )(value)
-
-
-def spread(sel):
-    eye = jnp.eye(G, dtype=BF16)
-    return (sel[:, None, :, None] * eye[None, :, None, :]).reshape(NB * G, TD * G)
+    )(weights, mixed, inverse)
 
 
 def local(matrix, mixers, bucket_pair, mixer_index, sign_seed):
-    mixed = mix(mixer_index, sign_seed, matrix, mixers)
-    flip = (1 - 2 * (sign_seed >> 29 & 1)).astype(F32)
-    bucket = jnp.arange(NB, dtype=jnp.int32)[:, None]
-    sel = (bucket == bucket_pair[:, 0]).astype(F32) + flip * (bucket == bucket_pair[:, 1]).astype(F32)
-    sel = sel.astype(BF16)
-    panel, other = scatter(mixed, jnp.pad(sel, ((0, 0), (0, HALF - TD))))
-    core = lax.axis_index("k")
-    mine = spread(sel)
-    theirs = spread(other[:, :TD])
-    both = jnp.where(core == 0, jnp.concatenate([mine, theirs], 1), jnp.concatenate([theirs, mine], 1))
-    part = jnp.dot(both, panel.reshape(NK * TD * G, HALF), preferred_element_type=F32)
-    sketch = total(part).reshape(NK, NB * G, HALF)
-    sketch = jnp.concatenate([sketch[0], sketch[1]], axis=1)
-    weight = jnp.dot(mine.T.astype(F32), sketch, precision=HI, preferred_element_type=F32)
-    gram_part = jnp.dot(sketch.T, sketch, precision=HI, preferred_element_type=F32)
-    weights, gram = share(weight, gram_part)
-    cross = jnp.dot(
-        weights.reshape(NC * TD * G, PS).T,
-        mixed.reshape(NC * TD * G, PS).astype(F32),
-        precision=HI,
-        preferred_element_type=F32,
-    )
-    factor = jnp.linalg.cholesky(gram)
-    solved = lax.linalg.triangular_solve(factor, cross, left_side=True, lower=True)
-    return finish(solved)
+    mixed, meta = mix(mixer_index, sign_seed, bucket_pair.reshape(-1), matrix, mixers)
+    panel, other = scatter(mixed, meta)
+    sketch = total(panel, meta, other)
+    weights, gram = share(sketch, meta)
+    return finish(weights, mixed, factor(gram))
 
 
 def solution(mesh):

time: 251 us -> 163 us (0.65)
  other arithmetic: 59.6 us -> 0 us
  local copies, waits for them, and re-layouts: 28.6 us -> 2.74 us
  matrix products: 10.9 us -> 0 us
  Pallas kernels: 150 us -> 160 us
    another operation x10 -> x0, other arithmetic: 54.6 us -> none  [the longest x6 34.2 us: local(): factor = jnp.linalg.cholesky(gram)]
    mul x3 -> x0, local copies, waits for them, and re-layouts: 20.7 us -> none  [spread(): sel[:, None, :, None] * eye[None, :, None, :]]
    pallas_call x3 -> x4, Pallas kernels: 74.4 us -> 84.5 us  [the longest x1 41.3 us: share(): pl.pallas_call(share_kernel, out_shape=(jax.ShapeDtypeStruct((NC, PS, TD...]
    dot_general x4 -> x0, matrix products: 9.58 us -> none  [the longest x1 5.65 us: local(): jnp.dot(weights.reshape(NC * TD * G, PS).T, mixed.reshape(NC * TD * G, PS...]
    mul x1 -> x0, other arithmetic: 4.24 us -> none  [spread(): sel[:, None, :, None] * eye[None, :, None, :]]
    another operation x9 -> x0, local copies, waits for them, and re-layouts: 4.07 us -> none
where the time goes in v2:
time: 163 us
  Pallas kernels  160 us (98%)
  local copies, waits for them, and re-layouts  2.74 us (2%)
    pallas_call x1, Pallas kernels, total(): pl.pallas_call(total_kernel, out_shape=jax.ShapeDtypeStruct((NK, NZ, rows...  44.7 us
    pallas_call x1, Pallas kernels, share(): pl.pallas_call(share_kernel, out_shape=(jax.ShapeDtypeStruct((NC, PS, TD...  41.3 us
    pallas_call x1, Pallas kernels, scatter(): pl.pallas_call(scatter_kernel, out_shape=(jax.ShapeDtypeStruct((NK, TD *...  30.7 us
    pallas_call x1, Pallas kernels, finish(): pl.pallas_call(finish_kernel, out_shape=jax.ShapeDtypeStruct((G, width),...  24 us
    pallas_call x1, Pallas kernels, factor(): pl.pallas_call(factor_kernel, out_shape=jax.ShapeDtypeStruct((PS, PS), F3...  11.7 us
    pallas_call x1, Pallas kernels, mix(): pl.pallas_call(mix_kernel, out_shape=(jax.ShapeDtypeStruct((TILE // G, TD...  7.44 us

profile of v2, /device:TPU:1, one launch (start us, length us, event | category | flops | bytes accessed | tf_op | source)
XLA Modules:
  0.0 162.6 jit_solution(14200161556478054086)
XLA Ops:
  0.0 0.8 copy.7
  0.8 0.7 reshape.3.pairs
  1.4 7.4 %mix.1 = (bf16[16,256,256]{2,1,0:T(8,128)(2,1)}, f32[8,256]{1,0:T(8,128)}) custom-call(s32[32]{0:T(128)} %which.1, s32[32]{0:T(128)} %seeds.1, s32[64]{0:T(128)} %reshape.3.pairs, f32[4096,256]{1,0:T(8,128)} %mat.1, f32[8,128,128]{2,1,0:T(8,128)} %mixers.1), custom_call_target="tpu_custom_call" | custom-call | tf_op jit(solution)/shard_map/mix/pallas_call | solution.py:86
  8.9 30.7 %scatter.1 = (bf16[2,256,128]{2,1,0:T(8,128)(2,1)}, f32[8,256]{1,0:T(8,128)}) custom-call(bf16[16,256,256]{2,1,0:T(8,128)(2,1)} %get-tuple-element.11.m_ref, f32[8,256]{1,0:T(8,128)} %get-tuple-element.12.sel_ref.mine_ref.meta_ref), custom_call_target="tpu_custom_call" | custom-call | tf_op jit(solution)/shard_map/scatter/pallas_call | solution.py:179
  39.6 44.7 %total.1.p_ref = f32[2,16,32,128]{3,2,1,0:T(8,128)} custom-call(bf16[2,256,128]{2,1,0:T(8,128)(2,1)} %get-tuple-element.13.x_ref, f32[8,256]{1,0:T(8,128)} %get-tuple-element.12.sel_ref.mine_ref.meta_ref, f32[8,256]{1,0:T(8,128)} %get-tuple-element.14.other_ref), custom_call_target="tpu_custom_call" | custom-call | tf_op jit(solution)/shard_map/total/pallas_call | solution.py:238
  84.3 41.3 %share.1 = (f32[16,256,256]{2,1,0:T(8,128)}, f32[256,256]{1,0:T(8,128)}) custom-call(f32[2,16,32,128]{3,2,1,0:T(8,128)} %total.1.p_ref, f32[8,256]{1,0:T(8,128)} %get-tuple-element.12.sel_ref.mine_ref.meta_ref), custom_call_target="tpu_custom_call" | custom-call | tf_op jit(solution)/shard_map/share/pallas_call | solution.py:390
  125.6 11.7 %factor.1.inv_ref = f32[256,256]{1,0:T(8,128)} custom-call(f32[256,256]{1,0:T(8,128)} %get-tuple-element.16.gram_ref), custom_call_target="tpu_custom_call" | custom-call | tf_op jit(solution)/shard_map/factor/pallas_call | solution.py:468
  137.3 24.0 %finish.1 = f32[8,256]{1,0:T(8,128)} custom-call(f32[16,256,256]{2,1,0:T(8,128)} %get-tuple-element.15.w_ref, bf16[16,256,256]{2,1,0:T(8,128)(2,1)} %get-tuple-element.11.m_ref, f32[256,256]{1,0:T(8,128)} %factor.1.inv_ref), custom_call_target="tpu_custom_call" | custom-call | tf_op jit(solution)/shard_map/finish/pallas_call | solution.py:522
  161.3 1.3 copy.9

commit v3 on v0

v3 whole, which is shorter than its diff:
```python
import functools

import jax
import jax.numpy as jnp
from jax import lax
from jax.experimental import pallas as pl
from jax.experimental.pallas import tpu as pltpu
from jax.sharding import Mesh
from jax.sharding import PartitionSpec as P

TILE = 128
PS = 256
NB = 64
TD = 32
NZ = 16
NK = 2
NX = 4
NC = 16
G = 8
HALF = 128
MESH = pl.DeviceIdType.MESH
HI = lax.Precision.HIGHEST
ROWS = ("z", "k")
COLS = ("x", "y")
F32 = jnp.float32
BF16 = jnp.bfloat16


def place():
    return tuple(lax.axis_index(a) for a in ("z", "k", "x", "y"))


def remote(src, dst, send, recv, to):
    return pltpu.make_async_remote_copy(
        src_ref=src, dst_ref=dst, send_sem=send, recv_sem=recv, device_id=to, device_id_type=MESH
    )


def hello(to):
    pl.semaphore_signal(pltpu.get_barrier_semaphore(), inc=1, device_id=to, device_id_type=MESH)


def meet(count):
    pl.semaphore_wait(pltpu.get_barrier_semaphore(), count)


def dot(a, b):
    return jnp.dot(a, b, precision=HI, preferred_element_type=F32)


def selection(meta):
    row = lax.broadcasted_iota(jnp.int32, (NB * G, TD * G), 0)
    lane = lax.broadcasted_iota(jnp.int32, (NB * G, TD * G), 1)
    first = meta[0:1, :].astype(jnp.int32)
    second = meta[1:2, :].astype(jnp.int32)
    flip = meta[2:3, :]
    bucket = row >> 3
    value = jnp.where(bucket == first, 1.0, 0.0) + jnp.where(bucket == second, flip, 0.0)
    return jnp.where((row & 7) == (lane & 7), value, 0.0).astype(BF16)


NBK = 64


def invert_block(block):
    n = NBK
    ident = (lax.broadcasted_iota(jnp.int32, (n, n), 0) == lax.broadcasted_iota(jnp.int32, (n, n), 1)).astype(F32)
    aug = jnp.concatenate([block, ident], axis=1)
    groups = n // G
    rows = [aug[g * G : (g + 1) * G, :] for g in range(groups)]
    sub = lax.broadcasted_iota(jnp.int32, (G, 2 * n), 0)
    for g in range(groups):
        cols = [
            {h: jnp.broadcast_to(rows[h][:, g * G + i : g * G + i + 1], (G, 2 * n)) for h in range(g, groups)}
            for i in range(G)
        ]
        scale = jnp.zeros((G, 2 * n), F32)
        for i in range(G):
            pivot = jnp.broadcast_to(cols[i][g][i : i + 1, :], (G, 2 * n))
            inv = 1.0 / pivot
            scale = jnp.where(sub == i, lax.rsqrt(pivot), scale)
            below = dict(cols[i])
            below[g] = jnp.where(sub > i, below[g], 0.0)
            for m in range(i + 1, G):
                f = jnp.broadcast_to(cols[m][g][i : i + 1, :], (G, 2 * n)) * inv
                for h in range(g, groups):
                    cols[m][h] = cols[m][h] - below[h] * f
            u = jnp.broadcast_to(rows[g][i : i + 1, :], (G, 2 * n)) * inv
            for h in range(g, groups):
                rows[h] = rows[h] - below[h] * u
        rows[g] = rows[g] * scale
    done = jnp.concatenate(rows, axis=0)
    return done[:, n:]


def start_factor(gram, work):
    work[:, :PS] = gram
    work[:, PS:] = (
        lax.broadcasted_iota(jnp.int32, (PS, PS), 0) == lax.broadcasted_iota(jnp.int32, (PS, PS), 1)
    ).astype(F32)


def factor_step(work, p):
    lo, hi = p * NBK, (p + 1) * NBK
    inv = invert_block(work[lo:hi, lo:hi])
    row = dot(inv, work[lo:hi, :])
    work[lo:hi, :] = row
    if hi < PS:
        work[hi:, :] = work[hi:, :] - dot(row[:, hi:PS].T, row)


VM = pl.BlockSpec(memory_space=pltpu.VMEM)
SM = pl.BlockSpec(memory_space=pltpu.SMEM)
DMA = pltpu.SemaphoreType.DMA
STEP_TILES = 8
QUARTER = PS // 4
OWN_ROWS = NB * G // NZ
RELAYS = ((4, (8, 5, 7)), (12, (14, 13, 15)), (1, (10, 9, 2)), (3, (6, 11)))


def mix_tiles(which, seeds, pairs, mat, mixers, m_ref, meta_ref):
    lane = lax.broadcasted_iota(jnp.int32, (1, TILE), 1) * 40503

    def some(step, carry):
        for pair in range(STEP_TILES // 2):
            parts = []
            for q in range(2):
                tile = step * STEP_TILES + 2 * pair + q
                hashed = (seeds[tile] ^ lane) * 69069
                sign = (1 - 2 * ((hashed >> 16) & 1)).astype(F32)
                mixer = mixers[which[tile]] * sign
                block = mat[pl.ds(pl.multiple_of(tile * TILE, TILE), TILE), :]
                parts.append(dot(mixer, block).reshape(TILE // G, G, mat.shape[1]))
            at = pl.multiple_of((step * STEP_TILES + 2 * pair) * G, 2 * G)
            m_ref[:, pl.ds(at, 2 * G), :] = jnp.concatenate(parts, axis=1).astype(BF16)
        return carry

    lax.fori_loop(0, TD // STEP_TILES, some, 0)
    tiles = lax.broadcasted_iota(jnp.int32, (1, TD * G), 1) // G
    first = jnp.zeros((1, TD * G), jnp.int32)
    second, seed = first, first
    for t in range(TD):
        first = jnp.where(tiles == t, pairs[t, 0], first)
        second = jnp.where(tiles == t, pairs[t, 1], second)
        seed = jnp.where(tiles == t, seeds[t], seed)
    flip = 1 - 2 * (seed >> 29 & 1)
    row = lax.broadcasted_iota(jnp.int32, (G, TD * G), 0)
    meta_ref[...] = jnp.where(row == 0, first, jnp.where(row == 1, second, flip)).astype(F32)


def main_kernel(
    which, seeds, pairs, mat, mixers, o_ref,
    m_ref, meta_ref, other_ref, x_ref, relay, y_ref, got_y, p_ref,
    w_ref, all_ref, g_ref, got_g, gram_ref, work, value, summed, pair, got_v,
    meta_sems, send_x, recv_x, send_r, recv_r,
    send_a, recv_a, send_b, recv_b, send_c, recv_c,
    send_w, recv_w, send_g, recv_g, send_h, recv_h,
    pair_sems, send_v, recv_v,
):
    z, k, x, y = place()
    col = x * NX + y
    source = col == 0
    sibling = {"k": 1 - k}

    def plane(d):
        other = lax.rem(k * NC + col + d, NK * NC)
        c = lax.rem(other, NC)
        return other // NC, c, {"k": other // NC, "x": c // NX, "y": lax.rem(c, NX)}

    def up(d):
        return lax.rem(z + d, NZ)

    for d in range(1, NK * NC):
        hello(plane(d)[2])
    for d in range(1, NZ):
        hello({"z": up(d)})
    mix_tiles(which, seeds, pairs, mat, mixers, m_ref, meta_ref)
    meet(NK * NC - 1 + NZ - 1)

    sent = []

    def go(copy):
        copy.start()
        sent.append(copy)

    def landed(ref, recv):
        remote(ref, ref, send_x.at[0, 0], recv, sibling).wait_recv()

    def half(c, kd):
        return m_ref.at[c, :, kd * HALF : (kd + 1) * HALF]

    def spot(c):
        return {"x": c // NX, "y": c % NX}

    pieces = []
    for j in range(3):
        for first, rest in RELAYS:
            if j < len(rest):
                for kd in range(NK):
                    c = rest[j]
                    pieces.append((half(c, kd), relay.at[j, kd], send_x.at[c, kd], recv_r.at[j, kd], spot(first)))
    for first, rest in RELAYS:
        for kd in range(NK):
            pieces.append(
                (half(first, kd), x_ref.at[k], send_x.at[first, kd], recv_x.at[k], {"k": kd, **spot(first)})
            )
    cross_half = m_ref.at[0, :, pl.ds(pl.multiple_of((1 - k) * HALF, HALF), HALF)]
    pieces.append((cross_half, x_ref.at[k], send_x.at[0, 0], recv_x.at[k], sibling))

    @pl.when(source)
    def _():
        for piece in pieces:
            remote(*piece).start()
        x_ref[k] = jnp.where(k == 0, m_ref[0, :, :HALF], m_ref[0, :, HALF:])

    go(remote(meta_ref, other_ref, meta_sems.at[0], meta_sems.at[1], sibling))

    def onward(j, kd, c):
        return remote(relay.at[j, kd], x_ref.at[k], send_r.at[j, kd], recv_x.at[k], {"k": kd, **spot(c)})

    for first, rest in RELAYS:
        @pl.when(col == first)
        def _():
            for j, c in enumerate(rest):
                for kd in range(NK):
                    landed(relay.at[j, kd], recv_r.at[j, kd])
                    onward(j, kd, c).start()

    landed(other_ref, meta_sems.at[1])
    mine = selection(meta_ref[...])
    theirs = selection(other_ref[...])

    @pl.when(jnp.logical_not(source))
    def _():
        landed(x_ref.at[k], recv_x.at[k])

    landed(x_ref.at[1 - k], recv_x.at[1 - k])
    part = jnp.dot(mine, x_ref[k], preferred_element_type=F32)
    part = part + jnp.dot(theirs, x_ref[1 - k], preferred_element_type=F32)
    y_ref[...] = part.reshape(y_ref.shape)

    for d in range(1, NZ):
        go(remote(y_ref.at[up(d)], got_y.at[d - 1], send_a.at[d - 1], recv_a.at[d - 1], {"z": up(d)}))
    acc = y_ref[z]
    for d in range(1, NZ):
        landed(got_y.at[d - 1], recv_a.at[d - 1])
        acc = acc + got_y[d - 1]
    p_ref[k, z] = acc
    for d in range(1, NZ):
        go(remote(p_ref.at[k, z], p_ref.at[k, z], send_b.at[d - 1], recv_b.at[d - 1], {"z": up(d)}))
    go(remote(p_ref.at[k, z], p_ref.at[k, z], send_c.at[0], recv_c.at[0], sibling))
    for d in range(1, NZ):
        zs = up(NZ - d)
        landed(p_ref.at[k, zs], recv_b.at[d - 1])
        go(remote(p_ref.at[k, zs], p_ref.at[k, zs], send_c.at[d], recv_c.at[d], sibling))
    for d in range(NZ):
        landed(p_ref.at[1 - k, up(NZ - d)], recv_c.at[d])

    sketch = jnp.concatenate([p_ref[0].reshape(NB * G, HALF), p_ref[1].reshape(NB * G, HALF)], axis=1)
    turned = sketch.T
    g_ref[...] = dot(turned, sketch)
    w_ref[...] = dot(turned, selection(meta_ref[...]).astype(F32))

    def rows_of(kk, c):
        return pl.ds(pl.multiple_of(kk * HALF + c * G, G), G)

    for d in range(1, NC):
        c = lax.rem(col + d, NC)
        go(
            remote(
                g_ref.at[rows_of(k, c), :], got_g.at[d - 1], send_g.at[d - 1], recv_g.at[d - 1],
                {"x": c // NX, "y": lax.rem(c, NX)},
            )
        )

    def piece_of(h, s):
        return pl.ds((2 * h + s) * QUARTER, QUARTER)

    def index(h, a, b):
        if h == 0:
            return lax.rem(x + a, NX) * NX + lax.rem(y + b, NX)
        return lax.rem(x + b, NX) * NX + lax.rem(y + a, NX)

    def send(h, a, b, s, stage, direction):
        c = index(h, a, b)
        there = all_ref.at[c, piece_of(h, s), :]
        here = w_ref.at[piece_of(h, s), :] if a == b == 0 else there
        step = 1 if direction == 0 else NX - 1
        to = {"x": lax.rem(x + step, NX)} if (h == 0) == (stage == 0) else {"y": lax.rem(y + step, NX)}
        go(remote(here, there, send_w.at[h, c, s, stage, direction], recv_w.at[h, c, s], to))

    seen = {(h, 0, 0, s) for h in range(2) for s in range(2)}

    def arrived(h, a, b, s):
        if (h, a, b, s) not in seen:
            seen.add((h, a, b, s))
            c = index(h, a, b)
            landed(all_ref.at[c, piece_of(h, s), :], recv_w.at[h, c, s])

    def across(h, a, s):
        arrived(h, a, 0, s)
        send(h, a, 0, s, 1, s)
        send(h, a, 0, s, 1, 1 - s)

    def pass_on(a):
        for h in range(2):
            arrived(h, a, 3, 0)
            send(h, a, 3, 0, 1, 0)
            arrived(h, a, 1, 1)
            send(h, a, 1, 1, 1, 1)

    for stage in range(2):
        for turn in range(2):
            for s in range(2):
                for h in range(2):
                    send(h, 0, 0, s, stage, s if turn == 0 else 1 - s)

    acc = g_ref[rows_of(k, col), :]
    for d in range(1, NC):
        landed(got_g.at[d - 1], recv_g.at[d - 1])
        acc = acc + got_g[d - 1]
    gram_ref[rows_of(k, col), :] = acc
    for d in range(1, NK * NC):
        own = gram_ref.at[rows_of(k, col), :]
        go(remote(own, own, send_h.at[d - 1], recv_h.at[d - 1], plane(d)[2]))

    for h in range(2):
        arrived(h, 3, 0, 0)
        send(h, 3, 0, 0, 0, 0)
        arrived(h, 1, 0, 1)
        send(h, 1, 0, 1, 0, 1)
    for a, s in ((3, 0), (1, 1), (3, 1), (1, 0)):
        for h in range(2):
            across(h, a, s)
    for d in range(1, NK * NC):
        kk, c, _ = plane(NK * NC - d)
        landed(gram_ref.at[rows_of(kk, c), :], recv_h.at[d - 1])
    all_ref[col] = w_ref[...]
    start_factor(gram_ref[...], work)
    factor_step(work, 0)
    for h in range(2):
        for s in range(2):
            across(h, 2, s)
    pass_on(0)
    factor_step(work, 1)
    pass_on(3)
    pass_on(1)
    factor_step(work, 2)
    pass_on(2)
    factor_step(work, 3)

    def ready(dx, dy):
        for s in range(2):
            arrived(0, dx, dy, s)
            arrived(1, dy, dx, s)

    def add(dx, dy, acc):
        c = lax.rem(x + dx, NX) * NX + lax.rem(y + dy, NX)
        w = all_ref[c]
        high = w.astype(BF16)
        rest = w - high.astype(F32)
        low = rest.astype(BF16)
        last = (rest - low.astype(F32)).astype(BF16)
        tiles = m_ref[c]
        for part in (high, low, last):
            acc = acc + jnp.dot(part, tiles, preferred_element_type=F32)
        return acc

    cross = jnp.zeros((PS, m_ref.shape[2]), F32)
    for d in range(NX):
        ready(d, 0)
        ready(0, d)
    cross = lax.fori_loop(
        0, 2 * NX - 1, lambda j, acc: add(jnp.where(j < NX, j, 0), jnp.where(j < NX, 0, j - NX + 1), acc), cross
    )
    for dx in range(1, NX):
        for dy in range(1, NX):
            ready(dx, dy)
    cross = lax.fori_loop(0, (NX - 1) ** 2, lambda j, acc: add(1 + j // 3, 1 + lax.rem(j, 3), acc), cross)
    value[...] = dot(work[:, PS:], cross).reshape(value.shape)
    go(remote(value.at[:, 1 - k], pair, pair_sems.at[0], pair_sems.at[1], sibling))
    landed(pair, pair_sems.at[1])
    summed[...] = value[:, k] + pair[...]
    for d in range(1, NZ):
        go(remote(summed.at[up(d)], got_v.at[d - 1], send_v.at[d - 1], recv_v.at[d - 1], {"z": up(d)}))
    acc = summed[z]
    for d in range(1, NZ):
        landed(got_v.at[d - 1], recv_v.at[d - 1])
        acc = acc + got_v[d - 1]
    o_ref[...] = acc

    @pl.when(source)
    def _():
        for piece in pieces:
            remote(*piece).wait_send()

    for first, rest in RELAYS:
        @pl.when(col == first)
        def _():
            for j, c in enumerate(rest):
                for kd in range(NK):
                    onward(j, kd, c).wait_send()

    for copy in sent:
        copy.wait_send()


def local(matrix, mixers, bucket_pair, mixer_index, sign_seed):
    width = matrix.shape[1]
    one, two, plane = (NZ - 1,), (2,), (NK * NC - 1,)
    return pl.pallas_call(
        main_kernel,
        out_shape=jax.ShapeDtypeStruct((G, width), F32),
        in_specs=[SM, SM, SM, VM, VM],
        out_specs=VM,
        scratch_shapes=[
            pltpu.VMEM((NC, TD * G, width), BF16),
            pltpu.VMEM((G, TD * G), F32),
            pltpu.VMEM((G, TD * G), F32),
            pltpu.VMEM((NK, TD * G, HALF), BF16),
            pltpu.VMEM((3, NK, TD * G, HALF), BF16),
            pltpu.VMEM((NZ, OWN_ROWS, HALF), F32),
            pltpu.VMEM((NZ - 1, OWN_ROWS, HALF), F32),
            pltpu.VMEM((NK, NZ, OWN_ROWS, HALF), F32),
            pltpu.VMEM((PS, TD * G), F32),
            pltpu.VMEM((NC, PS, TD * G), F32),
            pltpu.VMEM((PS, PS), F32),
            pltpu.VMEM((NC - 1, G, PS), F32),
            pltpu.VMEM((PS, PS), F32),
            pltpu.VMEM((PS, 2 * PS), F32),
            pltpu.VMEM((NZ, NK, G, width), F32),
            pltpu.VMEM((NZ, G, width), F32),
            pltpu.VMEM((NZ, G, width), F32),
            pltpu.VMEM((NZ - 1, G, width), F32),
            DMA(two), DMA((NC, NK)), DMA(two), DMA((3, NK)), DMA((3, NK)),
            DMA(one), DMA(one), DMA(one), DMA(one), DMA((NZ,)), DMA((NZ,)),
            DMA((2, NC, 2, 2, 2)), DMA((2, NC, 2)), DMA((NC - 1,)), DMA((NC - 1,)), DMA(plane), DMA(plane),
            DMA(two), DMA(one), DMA(one),
        ],
        compiler_params=pltpu.CompilerParams(collective_id=1, has_side_effects=True),
        name="main",
    )(mixer_index, sign_seed, bucket_pair, matrix, mixers)


def solution(mesh):
    split = Mesh(mesh.devices.reshape(NZ, NK, NX, NX), ("z", "k", "x", "y"))
    return jax.shard_map(
        local,
        mesh=split,
        in_specs=(P(ROWS, COLS), P(), P(ROWS, None), P(ROWS), P(ROWS)),
        out_specs=P(ROWS, COLS),
        check_vma=False,
    )
```

time: 731 us -> 119 us (0.16)
  blocking collectives: 387 us -> 0 us
  waiting for transfers between devices: 237 us -> 0 us
  Pallas kernels: 0 us -> 116 us
  other arithmetic: 62.5 us -> 0 us
  matrix products: 16.7 us -> 0 us
  between operations: 14.6 us -> 0.01 us
  local copies, waits for them, and re-layouts: 12 us -> 2.65 us
    all_to_all x1 -> x0, blocking collectives: 387 us -> none  [local(): lax.all_to_all(summed, ROWS, split_axis=1, concat_axis=0, tiled=True)]
    psum x2 -> x0, waiting for transfers between devices: 179 us -> none  [by_axis(): value = lax.psum(value, axis)]
    pallas_call x0 -> x1, Pallas kernels: none -> 116 us  [local(): pl.pallas_call(main_kernel, out_shape=jax.ShapeDtypeStruct((G, width), F3...]
    all_gather x1 -> x0, waiting for transfers between devices: 58.3 us -> none  [picked(): lax.all_gather(value, axis)]
    another operation x10 -> x0, other arithmetic: 54.3 us -> none  [the longest x6 34 us: local(): factor = jnp.linalg.cholesky(gram_total)]
    dot_general x4 -> x0, matrix products: 14.5 us -> none  [the longest x1 6.52 us: local(): jnp.einsum('tij,tjc->tic', chosen, row_sign[:, :, None] * blocks, precisi...]
  transfers between devices with their start and end apart: 3 -> 0, of which waited for: 3 -> 0; matrix products, arithmetic and copies ran while one was open for 0% -> 0% of each run, Pallas kernels for 0% -> 0%
where the time goes in v3:
time: 119 us
  Pallas kernels  116 us (97%)
  local copies, waits for them, and re-layouts  2.65 us (2%)
    pallas_call x1, Pallas kernels, local(): pl.pallas_call(main_kernel, out_shape=jax.ShapeDtypeStruct((G, width), F3...  116 us
    unnamed x2, local copies, waits for them, and re-layouts  2.65 us

profile of v3, /device:TPU:1, one launch (start us, length us, event | category | flops | bytes accessed | tf_op | source)
XLA Modules:
  0.0 118.6 jit_solution(6612881120666688032)
XLA Ops:
  0.0 1.4 %copy.6.pairs = s32[32,2]{1,0:T(8,128)} copy(s32[32,2]{0,1:T(2,128)} %param.7) | data formatting | bytes 512 | tf_op args[2]
  1.4 116.0 %main.1 = f32[8,256]{1,0:T(8,128)} custom-call(s32[32]{0:T(128)} %which.1, s32[32]{0:T(128)} %seeds.1, s32[32,2]{1,0:T(8,128)} %copy.6.pairs, f32[4096,256]{1,0:T(8,128)} %mat.1, f32[8,128,128]{2,1,0:T(8,128)} %mixers.1), custom_call_target="tpu_custom_call" | custom-call | tf_op jit(solution)/shard_map/main/pallas_call | solution.py:411
  117.3 1.3 %copy.8 = f32[8,256]{1,0:T(8,128)} copy(f32[8,256]{1,0:T(8,128)} %main.1) | data formatting | bytes 16384

commit v4 on v3

--- a/solution.py
+++ b/solution.py
@@ -110,12 +110,27 @@
 
 
 VM = pl.BlockSpec(memory_space=pltpu.VMEM)
-SM = pl.BlockSpec(memory_space=pltpu.SMEM)
+ANY = pl.BlockSpec(memory_space=pl.ANY)
 DMA = pltpu.SemaphoreType.DMA
 STEP_TILES = 8
 QUARTER = PS // 4
 OWN_ROWS = NB * G // NZ
+TINY = 1e-30
+FULL = 32767.0
+FAR_FIRST = sorted(range(1, NZ), key=lambda d: -min(d, NZ - d))
 RELAYS = ((4, (8, 5, 7)), (12, (14, 13, 15)), (1, (10, 9, 2)), (3, (6, 11)))
+
+
+def to_code(value):
+    return jnp.floor(value + 0.5).astype(jnp.int32).astype(jnp.int16)
+
+
+def from_code(code):
+    return code.astype(jnp.int32).astype(F32)
+
+
+def top_of(value):
+    return jnp.maximum(jnp.max(jnp.abs(value), axis=0, keepdims=True), TINY)
 
 
 def mix_tiles(which, seeds, pairs, mat, mixers, m_ref, meta_ref):
@@ -140,8 +155,8 @@
     first = jnp.zeros((1, TD * G), jnp.int32)
     second, seed = first, first
     for t in range(TD):
-        first = jnp.where(tiles == t, pairs[t, 0], first)
-        second = jnp.where(tiles == t, pairs[t, 1], second)
+        first = jnp.where(tiles == t, pairs[0, t], first)
+        second = jnp.where(tiles == t, pairs[1, t], second)
         seed = jnp.where(tiles == t, seeds[t], seed)
     flip = 1 - 2 * (seed >> 29 & 1)
     row = lax.broadcasted_iota(jnp.int32, (G, TD * G), 0)
@@ -149,11 +164,13 @@
 
 
 def main_kernel(
-    which, seeds, pairs, mat, mixers, o_ref,
-    m_ref, meta_ref, other_ref, x_ref, relay, y_ref, got_y, p_ref,
-    w_ref, all_ref, g_ref, got_g, gram_ref, work, value, summed, pair, got_v,
+    which_in, seeds_in, pairs_in, mat_in, mixers_in, o_ref,
+    which, seeds, pairs, mat, mixers, in_sems,
+    m_ref, meta_ref, other_ref, x_ref, relay, y_ref, yq_ref, ys_ref, got_y, got_s, pq_ref, ps_ref,
+    top_ref, got_t, w_ref, all_ref, g_ref, got_g, gram_ref, work, value, summed, pair, got_v,
     meta_sems, send_x, recv_x, send_r, recv_r,
     send_a, recv_a, send_b, recv_b, send_c, recv_c,
+    send_as, recv_as, send_bs, recv_bs, send_cs, recv_cs, send_t, recv_t,
     send_w, recv_w, send_g, recv_g, send_h, recv_h,
     pair_sems, send_v, recv_v,
 ):
@@ -174,6 +191,16 @@
         hello(plane(d)[2])
     for d in range(1, NZ):
         hello({"z": up(d)})
+    loads = [
+        pltpu.make_async_copy(src, dst, in_sems.at[i])
+        for i, (src, dst) in enumerate(
+            ((which_in, which), (seeds_in, seeds), (pairs_in, pairs), (mixers_in, mixers), (mat_in, mat))
+        )
+    ]
+    for load in loads:
+        load.start()
+    for load in loads:
+        load.wait()
     mix_tiles(which, seeds, pairs, mat, mixers, m_ref, meta_ref)
     meet(NK * NC - 1 + NZ - 1)
 
@@ -238,40 +265,65 @@
     part = jnp.dot(mine, x_ref[k], preferred_element_type=F32)
     part = part + jnp.dot(theirs, x_ref[1 - k], preferred_element_type=F32)
     y_ref[...] = part.reshape(y_ref.shape)
-
-    for d in range(1, NZ):
-        go(remote(y_ref.at[up(d)], got_y.at[d - 1], send_a.at[d - 1], recv_a.at[d - 1], {"z": up(d)}))
+    top = top_of(part)
+    yq_ref[...] = to_code(part * (FULL / top)).reshape(yq_ref.shape)
+    ys_ref[...] = top * (1.0 / FULL)
+
+    for d in FAR_FIRST:
+        go(remote(yq_ref.at[up(d)], got_y.at[d - 1], send_a.at[d - 1], recv_a.at[d - 1], {"z": up(d)}))
+        go(remote(ys_ref, got_s.at[d - 1], send_as.at[d - 1], recv_as.at[d - 1], {"z": up(d)}))
     acc = y_ref[z]
-    for d in range(1, NZ):
+    for d in FAR_FIRST[::-1]:
         landed(got_y.at[d - 1], recv_a.at[d - 1])
-        acc = acc + got_y[d - 1]
-    p_ref[k, z] = acc
-    for d in range(1, NZ):
-        go(remote(p_ref.at[k, z], p_ref.at[k, z], send_b.at[d - 1], recv_b.at[d - 1], {"z": up(d)}))
-    go(remote(p_ref.at[k, z], p_ref.at[k, z], send_c.at[0], recv_c.at[0], sibling))
-    for d in range(1, NZ):
+        landed(got_s.at[d - 1], recv_as.at[d - 1])
+        acc = acc + from_code(got_y[d - 1]) * got_s[d - 1]
+    top = top_of(acc)
+    pq_ref[k, z] = to_code(acc * (FULL / top))
+    ps_ref[k, z] = top * (1.0 / FULL)
+
+    def both(kk, zs, i, sems, scale_sems, to):
+        go(remote(pq_ref.at[kk, zs], pq_ref.at[kk, zs], sems[0].at[i], sems[1].at[i], to))
+        go(remote(ps_ref.at[kk, zs], ps_ref.at[kk, zs], scale_sems[0].at[i], scale_sems[1].at[i], to))
+
+    for d in FAR_FIRST:
+        both(k, z, d - 1, (send_b, recv_b), (send_bs, recv_bs), {"z": up(d)})
+    both(k, z, 0, (send_c, recv_c), (send_cs, recv_cs), sibling)
+    for d in FAR_FIRST[::-1]:
         zs = up(NZ - d)
-        landed(p_ref.at[k, zs], recv_b.at[d - 1])
-        go(remote(p_ref.at[k, zs], p_ref.at[k, zs], send_c.at[d], recv_c.at[d], sibling))
-    for d in range(NZ):
-        landed(p_ref.at[1 - k, up(NZ - d)], recv_c.at[d])
-
-    sketch = jnp.concatenate([p_ref[0].reshape(NB * G, HALF), p_ref[1].reshape(NB * G, HALF)], axis=1)
+        landed(pq_ref.at[k, zs], recv_b.at[d - 1])
+        landed(ps_ref.at[k, zs], recv_bs.at[d - 1])
+        both(k, zs, d, (send_c, recv_c), (send_cs, recv_cs), sibling)
+    for d in [0] + FAR_FIRST[::-1]:
+        landed(pq_ref.at[1 - k, up(NZ - d)], recv_c.at[d])
+        landed(ps_ref.at[1 - k, up(NZ - d)], recv_cs.at[d])
+
+    sketch = jnp.concatenate(
+        [(from_code(pq_ref[kk]) * ps_ref[kk]).reshape(NB * G, HALF) for kk in range(NK)], axis=1
+    )
+    top_ref[...] = top_of(sketch)
+
+    def same_core(d):
+        c = lax.rem(col + d, NC)
+        return {"x": c // NX, "y": lax.rem(c, NX)}
+
+    for d in range(1, NC):
+        go(remote(top_ref, got_t.at[d - 1], send_t.at[d - 1], recv_t.at[d - 1], same_core(d)))
     turned = sketch.T
     g_ref[...] = dot(turned, sketch)
-    w_ref[...] = dot(turned, selection(meta_ref[...]).astype(F32))
 
     def rows_of(kk, c):
         return pl.ds(pl.multiple_of(kk * HALF + c * G, G), G)
 
     for d in range(1, NC):
-        c = lax.rem(col + d, NC)
-        go(
-            remote(
-                g_ref.at[rows_of(k, c), :], got_g.at[d - 1], send_g.at[d - 1], recv_g.at[d - 1],
-                {"x": c // NX, "y": lax.rem(c, NX)},
-            )
-        )
+        go(remote(g_ref.at[rows_of(k, lax.rem(col + d, NC)), :], got_g.at[d - 1], send_g.at[d - 1], recv_g.at[d - 1], same_core(d)))
+    weight = dot(turned, mine.astype(F32))
+    top = top_ref[...]
+    for d in range(1, NC):
+        landed(got_t.at[d - 1], recv_t.at[d - 1])
+        top = jnp.maximum(top, got_t[d - 1])
+    unit = top * (2.0 / (FULL - 1.0))
+    inverse = jnp.broadcast_to(1.0 / unit, (G, PS)).T[:, 0:1]
+    w_ref[...] = to_code(weight * inverse)
 
     def piece_of(h, s):
         return pl.ds((2 * h + s) * QUARTER, QUARTER)
@@ -356,13 +408,11 @@
 
     def add(dx, dy, acc):
         c = lax.rem(x + dx, NX) * NX + lax.rem(y + dy, NX)
-        w = all_ref[c]
+        w = from_code(all_ref[c])
         high = w.astype(BF16)
-        rest = w - high.astype(F32)
-        low = rest.astype(BF16)
-        last = (rest - low.astype(F32)).astype(BF16)
+        low = (w - high.astype(F32)).astype(BF16)
         tiles = m_ref[c]
-        for part in (high, low, last):
+        for part in (high, low):
             acc = acc + jnp.dot(part, tiles, preferred_element_type=F32)
         return acc
 
@@ -377,14 +427,14 @@
         for dy in range(1, NX):
             ready(dx, dy)
     cross = lax.fori_loop(0, (NX - 1) ** 2, lambda j, acc: add(1 + j // 3, 1 + lax.rem(j, 3), acc), cross)
-    value[...] = dot(work[:, PS:], cross).reshape(value.shape)
+    value[...] = dot(work[:, PS:] * unit, cross).reshape(value.shape)
     go(remote(value.at[:, 1 - k], pair, pair_sems.at[0], pair_sems.at[1], sibling))
     landed(pair, pair_sems.at[1])
     summed[...] = value[:, k] + pair[...]
-    for d in range(1, NZ):
+    for d in FAR_FIRST:
         go(remote(summed.at[up(d)], got_v.at[d - 1], send_v.at[d - 1], recv_v.at[d - 1], {"z": up(d)}))
     acc = summed[z]
-    for d in range(1, NZ):
+    for d in FAR_FIRST[::-1]:
         landed(got_v.at[d - 1], recv_v.at[d - 1])
         acc = acc + got_v[d - 1]
     o_ref[...] = acc
@@ -411,19 +461,31 @@
     return pl.pallas_call(
         main_kernel,
         out_shape=jax.ShapeDtypeStruct((G, width), F32),
-        in_specs=[SM, SM, SM, VM, VM],
+        in_specs=[ANY] * 5,
         out_specs=VM,
         scratch_shapes=[
+            pltpu.SMEM((TD,), jnp.int32),
+            pltpu.SMEM((TD,), jnp.int32),
+            pltpu.SMEM((2, TD), jnp.int32),
+            pltpu.VMEM(matrix.shape, F32),
+            pltpu.VMEM(mixers.shape, F32),
+            DMA((5,)),
             pltpu.VMEM((NC, TD * G, width), BF16),
             pltpu.VMEM((G, TD * G), F32),
             pltpu.VMEM((G, TD * G), F32),
             pltpu.VMEM((NK, TD * G, HALF), BF16),
             pltpu.VMEM((3, NK, TD * G, HALF), BF16),
             pltpu.VMEM((NZ, OWN_ROWS, HALF), F32),
-            pltpu.VMEM((NZ - 1, OWN_ROWS, HALF), F32),
-            pltpu.VMEM((NK, NZ, OWN_ROWS, HALF), F32),
-            pltpu.VMEM((PS, TD * G), F32),
-            pltpu.VMEM((NC, PS, TD * G), F32),
+            pltpu.VMEM((NZ, OWN_ROWS, HALF), jnp.int16),
+            pltpu.VMEM((1, HALF), F32),
+            pltpu.VMEM((NZ - 1, OWN_ROWS, HALF), jnp.int16),
+            pltpu.VMEM((NZ - 1, 1, HALF), F32),
+            pltpu.VMEM((NK, NZ, OWN_ROWS, HALF), jnp.int16),
+            pltpu.VMEM((NK, NZ, 1, HALF), F32),
+            pltpu.VMEM((1, PS), F32),
+            pltpu.VMEM((NC - 1, 1, PS), F32),
+            pltpu.VMEM((PS, TD * G), jnp.int16),
+            pltpu.VMEM((NC, PS, TD * G), jnp.int16),
             pltpu.VMEM((PS, PS), F32),
             pltpu.VMEM((NC - 1, G, PS), F32),
             pltpu.VMEM((PS, PS), F32),
@@ -434,12 +496,13 @@
             pltpu.VMEM((NZ - 1, G, width), F32),
             DMA(two), DMA((NC, NK)), DMA(two), DMA((3, NK)), DMA((3, NK)),
             DMA(one), DMA(one), DMA(one), DMA(one), DMA((NZ,)), DMA((NZ,)),
+            DMA(one), DMA(one), DMA(one), DMA(one), DMA((NZ,)), DMA((NZ,)), DMA((NC - 1,)), DMA((NC - 1,)),
             DMA((2, NC, 2, 2, 2)), DMA((2, NC, 2)), DMA((NC - 1,)), DMA((NC - 1,)), DMA(plane), DMA(plane),
             DMA(two), DMA(one), DMA(one),
         ],
         compiler_params=pltpu.CompilerParams(collective_id=1, has_side_effects=True),
         name="main",
-    )(mixer_index, sign_seed, bucket_pair, matrix, mixers)
+    )(mixer_index, sign_seed, bucket_pair.T, matrix, mixers)
 
 
 def solution(mesh):

time: 119 us -> 99.2 us (0.83)
  Pallas kernels: 116 us -> 97.7 us
  local copies, waits for them, and re-layouts: 2.65 us -> 1.3 us
    pallas_call x1, Pallas kernels: 116 us -> 97.7 us  [local(): pl.pallas_call(main_kernel, out_shape=jax.ShapeDtypeStruct((G, width), F3...]
    unnamed x2 -> x1, local copies, waits for them, and re-layouts: 2.65 us -> 1.3 us
where the time goes in v4:
time: 99.2 us; the launch traced here: 99 us
  Pallas kernels  97.7 us (98%)
  local copies, waits for them, and re-layouts  1.3 us (1%)
    pallas_call x1, Pallas kernels, local(): pl.pallas_call(main_kernel, out_shape=jax.ShapeDtypeStruct((G, width), F3...  97.7 us

profile of v4, /device:TPU:1, one launch (start us, length us, event | category | flops | bytes accessed | tf_op | source)
XLA Modules:
  0.0 99.0 jit_solution(1454861421661541141)
XLA Ops:
  0.0 97.7 %main.1 = f32[8,256]{1,0:T(8,128)} custom-call(s32[32]{0:T(128)} %which_in.1, s32[32]{0:T(128)} %seeds_in.1, s32[2,32]{1,0:T(2,128)} %bitcast.1, f32[4096,256]{1,0:T(8,128)} %mat_in.1, f32[8,128,128]{2,1,0:T(8,128)} %mixers_in.1), custom_call_target="tpu_custom_call" | custom-call | tf_op jit(solution)/shard_map/main/pallas_call | solution.py:461
  97.7 1.3 %copy.7 = f32[8,256]{1,0:T(8,128)} copy(f32[8,256]{1,0:T(8,128)} %main.1) | data formatting | bytes 16384

commit v5 on v4

--- a/solution.py
+++ b/solution.py
@@ -103,10 +103,11 @@
 def factor_step(work, p):
     lo, hi = p * NBK, (p + 1) * NBK
     inv = invert_block(work[lo:hi, lo:hi])
-    row = dot(inv, work[lo:hi, :])
-    work[lo:hi, :] = row
+    left, right = lo // HALF * HALF, PS + -(-hi // HALF) * HALF
+    row = dot(inv, work[lo:hi, left:right])
+    work[lo:hi, left:right] = row
     if hi < PS:
-        work[hi:, :] = work[hi:, :] - dot(row[:, hi:PS].T, row)
+        work[hi:, left:right] = work[hi:, left:right] - dot(row[:, hi - left : PS - left].T, row)
 
 
 VM = pl.BlockSpec(memory_space=pltpu.VMEM)
@@ -133,7 +134,7 @@
     return jnp.maximum(jnp.max(jnp.abs(value), axis=0, keepdims=True), TINY)
 
 
-def mix_tiles(which, seeds, pairs, mat, mixers, m_ref, meta_ref):
+def mix_tiles(which, seeds, mat, mixers, m_ref, part):
     lane = lax.broadcasted_iota(jnp.int32, (1, TILE), 1) * 40503
 
     def some(step, carry):
@@ -150,7 +151,11 @@
             m_ref[:, pl.ds(at, 2 * G), :] = jnp.concatenate(parts, axis=1).astype(BF16)
         return carry
 
-    lax.fori_loop(0, TD // STEP_TILES, some, 0)
+    steps = TD // STEP_TILES // 2
+    lax.fori_loop(part * steps, (part + 1) * steps, some, 0)
+
+
+def fill_meta(seeds, pairs, meta_ref):
     tiles = lax.broadcasted_iota(jnp.int32, (1, TD * G), 1) // G
     first = jnp.zeros((1, TD * G), jnp.int32)
     second, seed = first, first
@@ -166,11 +171,11 @@
 def main_kernel(
     which_in, seeds_in, pairs_in, mat_in, mixers_in, o_ref,
     which, seeds, pairs, mat, mixers, in_sems,
-    m_ref, meta_ref, other_ref, x_ref, relay, y_ref, yq_ref, ys_ref, got_y, got_s, pq_ref, ps_ref,
+    m_ref, meta_ref, other_ref, x_ref, relay, y_ref, yq_ref, ys_ref, got_y, pq_ref, ps_ref,
     top_ref, got_t, w_ref, all_ref, g_ref, got_g, gram_ref, work, value, summed, pair, got_v,
     meta_sems, send_x, recv_x, send_r, recv_r,
     send_a, recv_a, send_b, recv_b, send_c, recv_c,
-    send_as, recv_as, send_bs, recv_bs, send_cs, recv_cs, send_t, recv_t,
+    send_as, recv_as, send_bs, recv_bs, send_t, recv_t,
     send_w, recv_w, send_g, recv_g, send_h, recv_h,
     pair_sems, send_v, recv_v,
 ):
@@ -187,21 +192,30 @@
     def up(d):
         return lax.rem(z + d, NZ)
 
-    for d in range(1, NK * NC):
-        hello(plane(d)[2])
-    for d in range(1, NZ):
-        hello({"z": up(d)})
+    rows = TD * TILE // 2
     loads = [
         pltpu.make_async_copy(src, dst, in_sems.at[i])
         for i, (src, dst) in enumerate(
-            ((which_in, which), (seeds_in, seeds), (pairs_in, pairs), (mixers_in, mixers), (mat_in, mat))
+            (
+                (which_in, which),
+                (seeds_in, seeds),
+                (pairs_in, pairs),
+                (mixers_in, mixers),
+                (mat_in.at[:rows, :], mat.at[:rows, :]),
+                (mat_in.at[rows:, :], mat.at[rows:, :]),
+            )
         )
     ]
     for load in loads:
         load.start()
-    for load in loads:
+    for d in FAR_FIRST:
+        hello({"z": up(d)})
+    for d in range(1, NK * NC):
+        hello(plane(d)[2])
+    for load in loads[:-1]:
         load.wait()
-    mix_tiles(which, seeds, pairs, mat, mixers, m_ref, meta_ref)
+    mix_tiles(which, seeds, mat, mixers, m_ref, 0)
+    fill_meta(seeds, pairs, meta_ref)
     meet(NK * NC - 1 + NZ - 1)
 
     sent = []
@@ -211,94 +225,121 @@
         sent.append(copy)
 
     def landed(ref, recv):
-        remote(ref, ref, send_x.at[0, 0], recv, sibling).wait_recv()
-
-    def half(c, kd):
-        return m_ref.at[c, :, kd * HALF : (kd + 1) * HALF]
+        remote(ref, ref, send_x.at[0, 0, 0], recv, sibling).wait_recv()
+
+    part_rows = TD * G // 2
+
+    def rows_in(part):
+        return pl.ds(part * part_rows, part_rows)
+
+    def half(c, kd, part):
+        return m_ref.at[c, rows_in(part), kd * HALF : (kd + 1) * HALF]
+
+    def home(part):
+        return x_ref.at[k, rows_in(part), :]
 
     def spot(c):
         return {"x": c // NX, "y": c % NX}
 
-    pieces = []
-    for j in range(3):
+    pieces = ([], [])
+    for part in range(2):
+        for j in range(3):
+            for first, rest in RELAYS:
+                if j < len(rest):
+                    for kd in range(NK):
+                        c = rest[j]
+                        pieces[part].append(
+                            (half(c, kd, part), relay.at[j, kd, rows_in(part), :], send_x.at[c, kd, part],
+                             recv_r.at[j, kd, part], spot(first))
+                        )
         for first, rest in RELAYS:
-            if j < len(rest):
-                for kd in range(NK):
-                    c = rest[j]
-                    pieces.append((half(c, kd), relay.at[j, kd], send_x.at[c, kd], recv_r.at[j, kd], spot(first)))
-    for first, rest in RELAYS:
-        for kd in range(NK):
-            pieces.append(
-                (half(first, kd), x_ref.at[k], send_x.at[first, kd], recv_x.at[k], {"k": kd, **spot(first)})
-            )
-    cross_half = m_ref.at[0, :, pl.ds(pl.multiple_of((1 - k) * HALF, HALF), HALF)]
-    pieces.append((cross_half, x_ref.at[k], send_x.at[0, 0], recv_x.at[k], sibling))
+            for kd in range(NK):
+                pieces[part].append(
+                    (half(first, kd, part), home(part), send_x.at[first, kd, part], recv_x.at[k, part],
+                     {"k": kd, **spot(first)})
+                )
+        cross_half = m_ref.at[0, rows_in(part), pl.ds(pl.multiple_of((1 - k) * HALF, HALF), HALF)]
+        pieces[part].append((cross_half, home(part), send_x.at[0, 0, part], recv_x.at[k, part], sibling))
 
     @pl.when(source)
     def _():
-        for piece in pieces:
+        for piece in pieces[0]:
+            remote(*piece).start()
+
+    go(remote(meta_ref, other_ref, meta_sems.at[0], meta_sems.at[1], sibling))
+    loads[-1].wait()
+    mix_tiles(which, seeds, mat, mixers, m_ref, 1)
+
+    @pl.when(source)
+    def _():
+        for piece in pieces[1]:
             remote(*piece).start()
         x_ref[k] = jnp.where(k == 0, m_ref[0, :, :HALF], m_ref[0, :, HALF:])
 
-    go(remote(meta_ref, other_ref, meta_sems.at[0], meta_sems.at[1], sibling))
-
-    def onward(j, kd, c):
-        return remote(relay.at[j, kd], x_ref.at[k], send_r.at[j, kd], recv_x.at[k], {"k": kd, **spot(c)})
+    def onward(j, kd, part, c):
+        return remote(
+            relay.at[j, kd, rows_in(part), :], home(part), send_r.at[j, kd, part], recv_x.at[k, part],
+            {"k": kd, **spot(c)}
+        )
 
     for first, rest in RELAYS:
         @pl.when(col == first)
         def _():
-            for j, c in enumerate(rest):
-                for kd in range(NK):
-                    landed(relay.at[j, kd], recv_r.at[j, kd])
-                    onward(j, kd, c).start()
+            for part in range(2):
+                for j, c in enumerate(rest):
+                    for kd in range(NK):
+                        landed(relay.at[j, kd, rows_in(part), :], recv_r.at[j, kd, part])
+                        onward(j, kd, part, c).start()
 
     landed(other_ref, meta_sems.at[1])
     mine = selection(meta_ref[...])
     theirs = selection(other_ref[...])
 
-    @pl.when(jnp.logical_not(source))
-    def _():
-        landed(x_ref.at[k], recv_x.at[k])
-
-    landed(x_ref.at[1 - k], recv_x.at[1 - k])
-    part = jnp.dot(mine, x_ref[k], preferred_element_type=F32)
-    part = part + jnp.dot(theirs, x_ref[1 - k], preferred_element_type=F32)
+    part = jnp.zeros((NB * G, HALF), F32)
+    for p in range(2):
+        @pl.when(jnp.logical_not(source))
+        def _():
+            landed(x_ref.at[k, rows_in(p), :], recv_x.at[k, p])
+
+        landed(x_ref.at[1 - k, rows_in(p), :], recv_x.at[1 - k, p])
+        span = slice(p * part_rows, (p + 1) * part_rows)
+        part = part + jnp.dot(mine[:, span], x_ref[k, span, :], preferred_element_type=F32)
+        part = part + jnp.dot(theirs[:, span], x_ref[1 - k, span, :], preferred_element_type=F32)
     y_ref[...] = part.reshape(y_ref.shape)
     top = top_of(part)
     yq_ref[...] = to_code(part * (FULL / top)).reshape(yq_ref.shape)
-    ys_ref[...] = top * (1.0 / FULL)
+    ys_ref[z] = top
 
     for d in FAR_FIRST:
         go(remote(yq_ref.at[up(d)], got_y.at[d - 1], send_a.at[d - 1], recv_a.at[d - 1], {"z": up(d)}))
-        go(remote(ys_ref, got_s.at[d - 1], send_as.at[d - 1], recv_as.at[d - 1], {"z": up(d)}))
+        go(remote(ys_ref.at[z], ys_ref.at[z], send_as.at[d - 1], recv_as.at[d - 1], {"z": up(d)}))
     acc = y_ref[z]
     for d in FAR_FIRST[::-1]:
+        zs = up(NZ - d)
         landed(got_y.at[d - 1], recv_a.at[d - 1])
-        landed(got_s.at[d - 1], recv_as.at[d - 1])
-        acc = acc + from_code(got_y[d - 1]) * got_s[d - 1]
-    top = top_of(acc)
+        landed(ys_ref.at[zs], recv_as.at[d - 1])
+        acc = acc + from_code(got_y[d - 1]) * (ys_ref[zs] * (1.0 / FULL))
+    top = ys_ref[0]
+    for other_z in range(1, NZ):
+        top = top + ys_ref[other_z]
+    top = top * 1.00001
     pq_ref[k, z] = to_code(acc * (FULL / top))
-    ps_ref[k, z] = top * (1.0 / FULL)
-
-    def both(kk, zs, i, sems, scale_sems, to):
-        go(remote(pq_ref.at[kk, zs], pq_ref.at[kk, zs], sems[0].at[i], sems[1].at[i], to))
-        go(remote(ps_ref.at[kk, zs], ps_ref.at[kk, zs], scale_sems[0].at[i], scale_sems[1].at[i], to))
+    ps_ref[k] = top * (1.0 / FULL)
+    go(remote(ps_ref.at[k], ps_ref.at[k], send_bs, recv_bs, sibling))
 
     for d in FAR_FIRST:
-        both(k, z, d - 1, (send_b, recv_b), (send_bs, recv_bs), {"z": up(d)})
-    both(k, z, 0, (send_c, recv_c), (send_cs, recv_cs), sibling)
+        go(remote(pq_ref.at[k, z], pq_ref.at[k, z], send_b.at[d - 1], recv_b.at[d - 1], {"z": up(d)}))
+    go(remote(pq_ref.at[k, z], pq_ref.at[k, z], send_c.at[0], recv_c.at[0], sibling))
     for d in FAR_FIRST[::-1]:
         zs = up(NZ - d)
         landed(pq_ref.at[k, zs], recv_b.at[d - 1])
-        landed(ps_ref.at[k, zs], recv_bs.at[d - 1])
-        both(k, zs, d, (send_c, recv_c), (send_cs, recv_cs), sibling)
+        go(remote(pq_ref.at[k, zs], pq_ref.at[k, zs], send_c.at[d], recv_c.at[d], sibling))
+    landed(ps_ref.at[1 - k], recv_bs)
     for d in [0] + FAR_FIRST[::-1]:
         landed(pq_ref.at[1 - k, up(NZ - d)], recv_c.at[d])
-        landed(ps_ref.at[1 - k, up(NZ - d)], recv_cs.at[d])
 
     sketch = jnp.concatenate(
-        [(from_code(pq_ref[kk]) * ps_ref[kk]).reshape(NB * G, HALF) for kk in range(NK)], axis=1
+        [from_code(pq_ref[kk]).reshape(NB * G, HALF) * ps_ref[kk] for kk in range(NK)], axis=1
     )
     top_ref[...] = top_of(sketch)
 
@@ -361,12 +402,13 @@
             arrived(h, a, 1, 1)
             send(h, a, 1, 1, 1, 1)
 
-    for stage in range(2):
+    def own_blocks(stage):
         for turn in range(2):
             for s in range(2):
                 for h in range(2):
                     send(h, 0, 0, s, stage, s if turn == 0 else 1 - s)
 
+    own_blocks(0)
     acc = g_ref[rows_of(k, col), :]
     for d in range(1, NC):
         landed(got_g.at[d - 1], recv_g.at[d - 1])
@@ -375,6 +417,7 @@
     for d in range(1, NK * NC):
         own = gram_ref.at[rows_of(k, col), :]
         go(remote(own, own, send_h.at[d - 1], recv_h.at[d - 1], plane(d)[2]))
+    own_blocks(1)
 
     for h in range(2):
         arrived(h, 3, 0, 0)
@@ -423,10 +466,11 @@
     cross = lax.fori_loop(
         0, 2 * NX - 1, lambda j, acc: add(jnp.where(j < NX, j, 0), jnp.where(j < NX, 0, j - NX + 1), acc), cross
     )
-    for dx in range(1, NX):
-        for dy in range(1, NX):
+    for offsets in (((1, 1), (1, 3), (3, 1), (3, 3)), ((1, 2), (3, 2), (2, 1), (2, 3)), ((2, 2),)):
+        for dx, dy in offsets:
             ready(dx, dy)
-    cross = lax.fori_loop(0, (NX - 1) ** 2, lambda j, acc: add(1 + j // 3, 1 + lax.rem(j, 3), acc), cross)
+        for dx, dy in offsets:
+            cross = add(dx, dy, cross)
     value[...] = dot(work[:, PS:] * unit, cross).reshape(value.shape)
     go(remote(value.at[:, 1 - k], pair, pair_sems.at[0], pair_sems.at[1], sibling))
     landed(pair, pair_sems.at[1])
@@ -441,15 +485,16 @@
 
     @pl.when(source)
     def _():
-        for piece in pieces:
+        for piece in pieces[0] + pieces[1]:
             remote(*piece).wait_send()
 
     for first, rest in RELAYS:
         @pl.when(col == first)
         def _():
-            for j, c in enumerate(rest):
-                for kd in range(NK):
-                    onward(j, kd, c).wait_send()
+            for part in range(2):
+                for j, c in enumerate(rest):
+                    for kd in range(NK):
+                        onward(j, kd, part, c).wait_send()
 
     for copy in sent:
         copy.wait_send()
@@ -469,7 +514,7 @@
             pltpu.SMEM((2, TD), jnp.int32),
             pltpu.VMEM(matrix.shape, F32),
             pltpu.VMEM(mixers.shape, F32),
-            DMA((5,)),
+            DMA((6,)),
             pltpu.VMEM((NC, TD * G, width), BF16),
             pltpu.VMEM((G, TD * G), F32),
             pltpu.VMEM((G, TD * G), F32),
@@ -477,11 +522,10 @@
             pltpu.VMEM((3, NK, TD * G, HALF), BF16),
             pltpu.VMEM((NZ, OWN_ROWS, HALF), F32),
             pltpu.VMEM((NZ, OWN_ROWS, HALF), jnp.int16),
-            pltpu.VMEM((1, HALF), F32),
+            pltpu.VMEM((NZ, 1, HALF), F32),
             pltpu.VMEM((NZ - 1, OWN_ROWS, HALF), jnp.int16),
-            pltpu.VMEM((NZ - 1, 1, HALF), F32),
             pltpu.VMEM((NK, NZ, OWN_ROWS, HALF), jnp.int16),
-            pltpu.VMEM((NK, NZ, 1, HALF), F32),
+            pltpu.VMEM((NK, 1, HALF), F32),
             pltpu.VMEM((1, PS), F32),
             pltpu.VMEM((NC - 1, 1, PS), F32),
             pltpu.VMEM((PS, TD * G), jnp.int16),
@@ -494,9 +538,9 @@
             pltpu.VMEM((NZ, G, width), F32),
             pltpu.VMEM((NZ, G, width), F32),
             pltpu.VMEM((NZ - 1, G, width), F32),
-            DMA(two), DMA((NC, NK)), DMA(two), DMA((3, NK)), DMA((3, NK)),
+            DMA(two), DMA((NC, NK, 2)), DMA((NK, 2)), DMA((3, NK, 2)), DMA((3, NK, 2)),
             DMA(one), DMA(one), DMA(one), DMA(one), DMA((NZ,)), DMA((NZ,)),
-            DMA(one), DMA(one), DMA(one), DMA(one), DMA((NZ,)), DMA((NZ,)), DMA((NC - 1,)), DMA((NC - 1,)),
+            DMA(one), DMA(one), DMA, DMA, DMA((NC - 1,)), DMA((NC - 1,)),
             DMA((2, NC, 2, 2, 2)), DMA((2, NC, 2)), DMA((NC - 1,)), DMA((NC - 1,)), DMA(plane), DMA(plane),
             DMA(two), DMA(one), DMA(one),
         ],

time: 99.2 us -> 96 us (0.968)
  Pallas kernels: 97.7 us -> 94.6 us
    pallas_call x1, Pallas kernels: 97.7 us -> 94.6 us  [local(): pl.pallas_call(main_kernel, out_shape=jax.ShapeDtypeStruct((G, width), F3...]
where the time goes in v5:
time: 96 us; the launch traced here: 95.9 us
  Pallas kernels  94.6 us (99%)
  local copies, waits for them, and re-layouts  1.3 us (1%)
    pallas_call x1, Pallas kernels, local(): pl.pallas_call(main_kernel, out_shape=jax.ShapeDtypeStruct((G, width), F3...  94.6 us

profile of v5, /device:TPU:1, one launch (start us, length us, event | category | flops | bytes accessed | tf_op | source)
XLA Modules:
  0.0 95.9 jit_solution(14241061460854769515)
XLA Ops:
  0.0 94.6 %main.1 = f32[8,256]{1,0:T(8,128)} custom-call(s32[32]{0:T(128)} %which_in.1, s32[32]{0:T(128)} %seeds_in.1, s32[2,32]{1,0:T(2,128)} %bitcast.1, f32[4096,256]{1,0:T(8,128)} %mat_in.1, f32[8,128,128]{2,1,0:T(8,128)} %mixers_in.1), custom_call_target="tpu_custom_call" | custom-call | tf_op jit(solution)/shard_map/main/pallas_call | solution.py:506
  94.6 1.3 %copy.7 = f32[8,256]{1,0:T(8,128)} copy(f32[8,256]{1,0:T(8,128)} %main.1) | data formatting | bytes 16384
